TPU v7x, 256 devices: a whole 4x4x8 slice. The times are simulated.
256 devices in a mesh: dev: 256 (over x, z, y, core).
Axes of the slice: x: 4, y: 4, z: 8, core: 2. Of those that a mesh axis runs over, the one named last changes fastest.
Arguments:
- contacts: bfloat16 [2048, 512, 512], P('dev'), as said below
- tile_count: int32 [256], replicated, may hold values from 1 to 8, as said below
- tile_row: int32 [2048], replicated, may hold values from 0 to 511, as said below
- tile_col: int32 [2048], replicated, may hold values from 0 to 511, as said below
- range_rows: int32 [256], replicated, may hold values from 1 to 4, as said below
Outputs:
- bias_one: float32 [256, 2048], P('dev')
- bias_two: float32 [256, 2048], P('dev')
- balanced: bfloat16 [2048, 512, 512], P('dev')
Inputs may be any that keep to these rules, and one draw needn't show every extreme that they name: `range_rows`: the ranges sum to 512 tile rows. tile_count[d] is 2 range_rows[d], less one on the last device; device d holds the blocks (r, r) and (r, r + 1) of the rows r of its own range, in its first tile_count[d] slots. `tile_row`: each block (r, r) and (r, r + 1) of the map is held in exactly one slot; slots that are not held have row block 0. `tile_col`: the column block of a held slot is its row block or the next one; slots that are not held have column block 0. `contacts`: entries are positive; a held tile whose row and column blocks are equal is symmetric.
All inputs are finite; a program needn't handle non-finite values.
Results may differ from a plain program's by a relative error of at most 0.001.
Values sent between devices are 32-bit elements; how exact they have to be, the bound alone decides.
No kernel may reach another device: no remote copies, remote signals or barrier semaphores. Data moves between devices by JAX's collectives and lax.ppermute only.
A program may use at most 64 MiB of HBM per device.

v0:
```python
import jax
import jax.numpy as jnp
from jax import lax
from jax.sharding import Mesh
from jax.sharding import PartitionSpec as P

TILE = 512
TR_DEV = 2
DEV = ("dev_0", "dev_1", "dev_2", "dev_3")


def from_behind(x, axis, by):
    count = lax.axis_size(axis)
    pairs = [(i, i + by) for i in range(count) if 0 <= i + by < count]
    return lax.ppermute(x, axis, pairs)


def from_everyone(x, axis):
    count = lax.axis_size(axis)
    return lax.all_to_all(jnp.broadcast_to(x[None], (count, *x.shape)), axis, 0, 0, tiled=True)


def of_everyone(x, axis):
    everything = from_everyone(x, axis)
    return jnp.sum(everything, axis=0)


def by_axis(x, axes):
    far, near = axes
    nearer = of_everyone(x, near)
    return of_everyone(nearer, far)


def shards(contacts, tile_count, tile_row, tile_col, range_rows):
    devices_total = lax.axis_size(DEV)
    dev_index = lax.axis_index(DEV)
    slot_count = contacts.shape[0]
    tile_size = contacts.shape[1]
    block_rows = TR_DEV * devices_total
    bin_total = block_rows * tile_size
    own_rows = lax.dynamic_slice_in_dim(tile_row, dev_index * slot_count, slot_count)
    own_cols = lax.dynamic_slice_in_dim(tile_col, dev_index * slot_count, slot_count)
    held_mask = (jnp.arange(slot_count) < tile_count[dev_index]).astype(jnp.float32)
    offdiag = (own_rows != own_cols).astype(jnp.float32)
    range_cap = 2 * TR_DEV * tile_size
    starts = jnp.cumsum(range_rows) - range_rows
    own_count = range_rows[dev_index]
    first_row = starts[dev_index]
    window_rows = slot_count // 2 + 1
    held = held_mask > 0
    local_row = jnp.where(held, own_rows - first_row, 0)
    local_col = jnp.where(held, own_cols - first_row, 0)
    row_ids = jnp.arange(window_rows)

    def scaled_local(window):
        inverse = 1.0 / window
        return (
            contacts.astype(jnp.float32)
            * inverse[local_row][:, :, None]
            * inverse[local_col][:, None, :]
        )

    def route_sweep(window):
        scaled = scaled_local(window)
        row_part = jnp.sum(scaled, 2) * held_mask[:, None]
        col_part = jnp.sum(scaled, 1) * (held_mask * offdiag)[:, None]
        local = (
            jnp.zeros((window_rows, tile_size), jnp.float32)
            .at[local_row]
            .add(row_part)
            .at[local_col]
            .add(col_part)
        )
        spill = lax.dynamic_index_in_dim(local, own_count, 0, keepdims=False)
        arrived = from_behind(spill, DEV, 1)
        whole_sum = by_axis(jnp.sum(local), (("dev_0", "dev_1"), ("dev_2", "dev_3")))
        sums = local.at[0].add(arrived)
        valid = (row_ids < own_count)[:, None]
        new_own = jnp.where(valid, window * (sums / (whole_sum / bin_total)), 1.0)
        next_first = from_behind(new_own[0], DEV, -1)
        next_first = jnp.where(dev_index == devices_total - 1, 1.0, next_first)
        return jnp.where((row_ids == own_count)[:, None], next_first[None, :], new_own)

    window_a = route_sweep(jnp.ones((window_rows, tile_size), jnp.float32))
    window_b = route_sweep(window_a)
    balanced = (scaled_local(window_b) * TILE * held_mask[:, None, None]).astype(jnp.bfloat16)

    def route_ranged(window):
        flat = window[: window_rows - 1].reshape(-1)
        return jnp.where(jnp.arange(range_cap) < own_count * tile_size, flat, 0.0)[None, :]

    return (route_ranged(window_a), route_ranged(window_b), balanced)


def solution(mesh):
    finer = Mesh(mesh.devices.reshape(4, 8, 4, 2), ("dev_0", "dev_1", "dev_2", "dev_3"))
    return jax.shard_map(
        shards,
        mesh=finer,
        in_specs=(P(DEV, None, None), P(), P(), P(), P()),
        out_specs=(P(DEV, None), P(DEV, None), P(DEV, None, None)),
        check_vma=False,
    )
```

profile of v0, /device:TPU:1, one launch (start us, length us, event | category | flops | bytes accessed | tf_op | source)
XLA Modules:
  0.0 102.8 jit_solution(3710677196359915069)
XLA Ops:
  0.6 0.0 copy-start
  0.7 1.3 %dynamic_slice.23 = s32[1]{0:T(128)} dynamic-slice(s32[256]{0:T(256)} %param.10, s32[]{:T(128)S(6)} %select_n.82), dynamic_slice_sizes={1} | dynamic-slice | bytes 12 | tf_op jit(solution)/shard_map/dynamic_slice | solution.py:43
  1.9 0.6 compare_convert_fusion
  2.6 1.0 reduce-window.9
  3.6 0.1 slice.53
  3.7 0.1 slice_reduce_fusion
  3.8 0.8 bitcast_subtract_fusion
  4.5 0.6 dynamic_slice.25
  5.1 1.4 %compare_select_fusion.4 = (f32[8]{0:T(128)S(1)}, f32[8]{0:T(128)S(1)}) fusion(s32[2048]{0:T(1024)} %param.12, s32[]{:T(128)S(6)} %select_n.84, s32[2048]{0:T(1024)} %param.11, s32[]{:T(128)} %bitcast.1), kind=kLoop, calls=%fused_computation.52 | loop fusion | flops 40 | bytes 136 | tf_op jit(solution)/shard_map/mul | solution.py:66
  6.5 2.1 %compare_select_fusion.2 = (s32[8]{0:T(128)S(1)}, s32[8]{0:T(128)S(1)}) fusion(s32[]{:T(128)} %bitcast.4, s32[2048]{0:T(1024)} %param.12, s32[]{:T(128)S(6)} %select_n.84, s32[]{:T(128)} %bitcast.1, s32[2048]{0:T(1024)} %param.11), kind=kLoop, calls=%fused_computation.48 | loop fusion | flops 104 | bytes 140 | tf_op jit(solution)/shard_map/select_n | solution.py:60
  8.7 0.6 gather_fusion.1
  9.2 0.6 gather_fusion
  9.8 3.6 %fusion.1 = (f32[8,512]{1,0:T(8,128)S(1)}, f32[8,512]{1,0:T(8,128)S(1)}) fusion(bf16[8,512,512]{2,1,0:T(8,128)(2,1)} %param.9, f32[8,512]{1,0:T(8,128)S(1)} %gather_fusion.1, f32[8,512]{1,0:T(8,128)S(1)} %gather_fusion), kind=kLoop, calls=%fused_computation.14 | loop fusion | flops 10477568 | bytes 4259840 | tf_op jit(solution)/shard_map/reduce_sum | solution.py:66
  13.4 0.7 scatter_custom_fusion
  14.1 0.7 scatter_custom_fusion.1
  14.9 0.6 reduce_sum.92
  15.5 1.2 %broadcast_in_dim.116 = f32[8,1,1]{2,1,0:T(1,128)} broadcast(f32[]{:T(128)} %reduce_sum.92), dimensions={} | broadcast | bytes 36 | tf_op jit(solution)/shard_map/broadcast_in_dim | solution.py:20
  16.7 6.4 %all-to-all-start = ((f32[8,1,1]{2,1,0:T(1,128)}), f32[8,1,1]{2,1,0:T(1,128)S(1)}, u32[]{:S(2)}, u32[]{:S(2)}) async-start(f32[8,1,1]{2,1,0:T(1,128)} %broadcast_in_dim.116), calls=%async_computation | async-start | bytes 8192 | tf_op jit(solution)/shard_map/all_to_all | solution.py:20
  23.1 0.0 copy-done
  23.1 0.6 dynamic_slice.22
  25.7 3.5 %collective-permute-start = (f32[512]{0:T(512)S(1)}, f32[512]{0:T(512)S(1)}, u32[]{:S(2)}, u32[]{:S(2)}) collective-permute-start(f32[512]{0:T(512)S(1)} %bitcast.26), channel_id=1, source_target_pairs={{0,1},{1,2},{2,3},{3,4},{4,5},{5,6},{6,7},{7,8},{8,9},{9,10},{10,1... | collective-permute-start | bytes 6152 | tf_op jit(solution)/shard_map/ppermute | solution.py:15
  29.2 0.0 all-to-all-done
  29.2 0.6 reduce_sum.93
  29.9 1.3 %broadcast_in_dim.117 = f32[32,1,1]{2,1,0:T(1,128)} broadcast(f32[]{:T(128)} %reduce_sum.93), dimensions={} | broadcast | bytes 132 | tf_op jit(solution)/shard_map/broadcast_in_dim | solution.py:20
  31.1 10.6 %all-to-all-start.1 = ((f32[32,1,1]{2,1,0:T(1,128)}), f32[32,1,1]{2,1,0:T(1,128)S(1)}, u32[]{:S(2)}, u32[]{:S(2)}) async-start(f32[32,1,1]{2,1,0:T(1,128)} %broadcast_in_dim.117), calls=%async_computation.1 | async-start | bytes 32768 | tf_op jit(solution)/shard_map/all_to_all | solution.py:20
  41.7 0.7 iota_compare_fusion
  42.4 8.0 %all-to-all-done.1 = f32[32,1,1]{2,1,0:T(1,128)S(1)} async-done(((f32[32,1,1]{2,1,0:T(1,128)}), f32[32,1,1]{2,1,0:T(1,128)S(1)}, u32[]{:S(2)}, u32[]{:S(2)}) %all-to-all-start.1) | async-done | bytes 160 | tf_op jit(solution)/shard_map/all_to_all | solution.py:20
  50.3 0.6 reduce_sum.94
  51.6 0.0 collective-permute-done
  51.6 0.1 scatter-add.40
  51.7 0.1 divide_select_fusion
  51.8 2.4 %collective-permute-start.1 = (f32[512]{0:T(512)S(1)}, f32[512]{0:T(512)S(1)}, u32[]{:S(2)}, u32[]{:S(2)}) collective-permute-start(f32[512]{0:T(512)S(1)} %bitcast.27), channel_id=1, source_target_pairs={{1,0},{2,1},{3,2},{4,3},{5,4},{6,5},{7,6},{8,7},{9,8},{10,9},{11,1... | collective-permute-start | bytes 6152 | tf_op jit(solution)/shard_map/ppermute | solution.py:15
  54.2 0.7 iota_compare_fusion.1
  55.5 1.2 %collective-permute-done.1 = f32[512]{0:T(512)S(1)} collective-permute-done((f32[512]{0:T(512)S(1)}, f32[512]{0:T(512)S(1)}, u32[]{:S(2)}, u32[]{:S(2)}) %collective-permute-start.1) | collective-permute-done | bytes 2080 | tf_op jit(solution)/shard_map/ppermute | solution.py:15
  56.7 0.1 broadcast_divide_fusion.1
  56.8 0.6 gather_fusion.3
  57.3 0.6 gather_fusion.2
  57.9 3.6 %fusion.4 = (f32[8,512]{1,0:T(8,128)S(1)}, f32[8,512]{1,0:T(8,128)S(1)}) fusion(bf16[8,512,512]{2,1,0:T(8,128)(2,1)} %param.9, f32[8,512]{1,0:T(8,128)S(1)} %gather_fusion.3, f32[8,512]{1,0:T(8,128)S(1)} %gather_fusion.2), kind=kLoop, calls=%fused_computation.17 | loop fusion | flops 10477568 | bytes 4259840 | tf_op jit(solution)/shard_map/reduce_sum | solution.py:66
  61.5 0.7 scatter_custom_fusion.2
  62.3 0.7 scatter_custom_fusion.3
  63.0 0.6 reduce_sum.97
  63.6 1.2 %broadcast_in_dim.120 = f32[8,1,1]{2,1,0:T(1,128)} broadcast(f32[]{:T(128)} %reduce_sum.97), dimensions={} | broadcast | bytes 36 | tf_op jit(solution)/shard_map/broadcast_in_dim | solution.py:20
  64.8 5.2 %all-to-all-start.2 = ((f32[8,1,1]{2,1,0:T(1,128)}), f32[8,1,1]{2,1,0:T(1,128)S(1)}, u32[]{:S(2)}, u32[]{:S(2)}) async-start(f32[8,1,1]{2,1,0:T(1,128)} %broadcast_in_dim.120), calls=%async_computation.2 | async-start | bytes 8192 | tf_op jit(solution)/shard_map/all_to_all | solution.py:20
  70.0 3.5 %collective-permute-start.2 = (f32[512]{0:T(512)S(1)}, f32[512]{0:T(512)S(1)}, u32[]{:S(2)}, u32[]{:S(2)}) collective-permute-start(f32[512]{0:T(512)S(1)} %bitcast.25), channel_id=1, source_target_pairs={{0,1},{1,2},{2,3},{3,4},{4,5},{5,6},{6,7},{7,8},{8,9},{9,10},{10,1... | collective-permute-start | bytes 6152 | tf_op jit(solution)/shard_map/ppermute | solution.py:15
  73.5 1.0 all-to-all-done.2
  74.5 0.6 reduce_sum.98
  75.1 1.3 %broadcast_in_dim.121 = f32[32,1,1]{2,1,0:T(1,128)} broadcast(f32[]{:T(128)} %reduce_sum.98), dimensions={} | broadcast | bytes 132 | tf_op jit(solution)/shard_map/broadcast_in_dim | solution.py:20
  76.4 4.7 %all-to-all-start.3 = ((f32[32,1,1]{2,1,0:T(1,128)}), f32[32,1,1]{2,1,0:T(1,128)S(1)}, u32[]{:S(2)}, u32[]{:S(2)}) async-start(f32[32,1,1]{2,1,0:T(1,128)} %broadcast_in_dim.121), calls=%async_computation.3 | async-start | bytes 32768 | tf_op jit(solution)/shard_map/all_to_all | solution.py:20
  81.1 8.6 %all-to-all-done.3 = f32[32,1,1]{2,1,0:T(1,128)S(1)} async-done(((f32[32,1,1]{2,1,0:T(1,128)}), f32[32,1,1]{2,1,0:T(1,128)S(1)}, u32[]{:S(2)}, u32[]{:S(2)}) %all-to-all-start.3) | async-done | bytes 160 | tf_op jit(solution)/shard_map/all_to_all | solution.py:20
  89.7 0.6 reduce_sum.99
  91.0 0.0 collective-permute-done.2
  91.0 0.1 scatter-add.43
  91.1 0.1 multiply_select_fusion
  91.1 4.0 %collective-permute-start.3 = (f32[512]{0:T(512)S(1)}, f32[512]{0:T(512)S(1)}, u32[]{:S(2)}, u32[]{:S(2)}) collective-permute-start(f32[512]{0:T(512)S(1)} %bitcast.28), channel_id=1, source_target_pairs={{1,0},{2,1},{3,2},{4,3},{5,4},{6,5},{7,6},{8,7},{9,8},{10,9},{11,1... | collective-permute-start | bytes 6152 | tf_op jit(solution)/shard_map/ppermute | solution.py:15
  95.2 0.6 compare_select_fusion.1
  95.8 0.8 collective-permute-done.3
  96.6 0.1 broadcast_divide_fusion
  96.7 0.6 gather_fusion.5
  97.2 0.6 gather_fusion.4
  97.8 0.6 compare_select_fusion
  98.5 4.3 %fusion.8 = bf16[8,512,512]{2,1,0:T(8,128)(2,1)} fusion(bf16[8,512,512]{2,1,0:T(8,128)(2,1)} %param.9, f32[8]{0:T(128)S(1)} %get-tuple-element.38, f32[8,512]{1,0:T(8,128)S(1)} %gather_fusion.5, f32[8,512]{1,0:T(8,128)S(1)} %gather_fusion.4), kind=kLoop, calls=%fused_computation.21 | loop fusion | flops 10485760 | bytes 8421408 | tf_op jit(solution)/shard_map/convert_element_type | solution.py:86
  (16 shorter events, 0.1 us)
Async XLA Ops:
  0.6 22.5 %copy-start = (s32[256]{0:T(256)S(1)}, s32[256]{0:T(256)}, u32[]{:S(2)}) copy-start(s32[256]{0:T(256)} %param.13) | copy-start | bytes 3076
  16.7 12.5 %all-to-all-start = ((f32[8,1,1]{2,1,0:T(1,128)}), f32[8,1,1]{2,1,0:T(1,128)S(1)}, u32[]{:S(2)}, u32[]{:S(2)}) async-start(f32[8,1,1]{2,1,0:T(1,128)} %broadcast_in_dim.116), calls=%async_computation | async-start | bytes 8192 | tf_op jit(solution)/shard_map/all_to_all | solution.py:20
  25.7 25.9 %collective-permute-start = (f32[512]{0:T(512)S(1)}, f32[512]{0:T(512)S(1)}, u32[]{:S(2)}, u32[]{:S(2)}) collective-permute-start(f32[512]{0:T(512)S(1)} %bitcast.26), channel_id=1, source_target_pairs={{0,1},{1,2},{2,3},{3,4},{4,5},{5,6},{6,7},{7,8},{8,9},{9,10},{10,1... | collective-permute-start | bytes 6152 | tf_op jit(solution)/shard_map/ppermute | solution.py:15
  31.1 19.2 %all-to-all-start.1 = ((f32[32,1,1]{2,1,0:T(1,128)}), f32[32,1,1]{2,1,0:T(1,128)S(1)}, u32[]{:S(2)}, u32[]{:S(2)}) async-start(f32[32,1,1]{2,1,0:T(1,128)} %broadcast_in_dim.117), calls=%async_computation.1 | async-start | bytes 32768 | tf_op jit(solution)/shard_map/all_to_all | solution.py:20
  51.8 4.9 %collective-permute-start.1 = (f32[512]{0:T(512)S(1)}, f32[512]{0:T(512)S(1)}, u32[]{:S(2)}, u32[]{:S(2)}) collective-permute-start(f32[512]{0:T(512)S(1)} %bitcast.27), channel_id=1, source_target_pairs={{1,0},{2,1},{3,2},{4,3},{5,4},{6,5},{7,6},{8,7},{9,8},{10,9},{11,1... | collective-permute-start | bytes 6152 | tf_op jit(solution)/shard_map/ppermute | solution.py:15
  64.8 9.7 %all-to-all-start.2 = ((f32[8,1,1]{2,1,0:T(1,128)}), f32[8,1,1]{2,1,0:T(1,128)S(1)}, u32[]{:S(2)}, u32[]{:S(2)}) async-start(f32[8,1,1]{2,1,0:T(1,128)} %broadcast_in_dim.120), calls=%async_computation.2 | async-start | bytes 8192 | tf_op jit(solution)/shard_map/all_to_all | solution.py:20
  70.0 21.0 %collective-permute-start.2 = (f32[512]{0:T(512)S(1)}, f32[512]{0:T(512)S(1)}, u32[]{:S(2)}, u32[]{:S(2)}) collective-permute-start(f32[512]{0:T(512)S(1)} %bitcast.25), channel_id=1, source_target_pairs={{0,1},{1,2},{2,3},{3,4},{4,5},{5,6},{6,7},{7,8},{8,9},{9,10},{10,1... | collective-permute-start | bytes 6152 | tf_op jit(solution)/shard_map/ppermute | solution.py:15
  76.4 13.3 %all-to-all-start.3 = ((f32[32,1,1]{2,1,0:T(1,128)}), f32[32,1,1]{2,1,0:T(1,128)S(1)}, u32[]{:S(2)}, u32[]{:S(2)}) async-start(f32[32,1,1]{2,1,0:T(1,128)} %broadcast_in_dim.121), calls=%async_computation.3 | async-start | bytes 32768 | tf_op jit(solution)/shard_map/all_to_all | solution.py:20
  91.1 5.5 %collective-permute-start.3 = (f32[512]{0:T(512)S(1)}, f32[512]{0:T(512)S(1)}, u32[]{:S(2)}, u32[]{:S(2)}) collective-permute-start(f32[512]{0:T(512)S(1)} %bitcast.28), channel_id=1, source_target_pairs={{1,0},{2,1},{3,2},{4,3},{5,4},{6,5},{7,6},{8,7},{9,8},{10,9},{11,1... | collective-permute-start | bytes 6152 | tf_op jit(solution)/shard_map/ppermute | solution.py:15
where the time goes:
time: 103 us
  starting transfers between devices  40.4 us (39%)
  other arithmetic  26.9 us (26%)
  waiting for transfers between devices  19.5 us (19%)
  local copies, waits for them, and re-layouts  11.2 us (11%)
  between operations  4.82 us (5%)
    all_to_all x4, starting transfers between devices, from_everyone(): lax.all_to_all(jnp.broadcast_to(x[None], (count, *x.shape)), axis, 0, 0,...  26.8 us
    all_to_all x4, waiting for transfers between devices, from_everyone(): lax.all_to_all(jnp.broadcast_to(x[None], (count, *x.shape)), axis, 0, 0,...  17.5 us
    ppermute x4, starting transfers between devices, from_behind(): return lax.ppermute(x, axis, pairs)  13.5 us
    reduce_sum x2, other arithmetic, route_sweep(): col_part = jnp.sum(scaled, 1) * (held_mask * offdiag)[:, None]  7.28 us
    broadcast_in_dim x4, local copies, waits for them, and re-layouts, from_everyone(): jnp.broadcast_to(x[None], (count, *x.shape))  5 us
    convert_element_type x1, other arithmetic, shards(): (scaled_local(window_b) * TILE * held_mask[:, None, None]).astype(jnp.bfl...  4.32 us
    scatter-add x4, other arithmetic, route_sweep(): local = jnp.zeros((window_rows, tile_size), jnp.float32).at[local_row].ad...  2.84 us
    reduce_sum x4, other arithmetic, of_everyone(): return jnp.sum(everything, axis=0)  2.49 us
  transfers between devices with their start and end apart: 8, of which 5 were waited for; matrix products, arithmetic and copies ran while one was open for 7% of the time, Pallas kernels for 0%

commit v1 on v0

v1 whole, which is shorter than its diff:
```python
import jax
import jax.numpy as jnp
from jax import lax
from jax.experimental import pallas as pl
from jax.experimental.pallas import tpu as pltpu
from jax.sharding import PartitionSpec as P

TILE = 512
SLOTS = 8
ROWS = 8
CAP = 4
DEVICES = 256
BINS = 262144
F32 = jnp.float32
BF16 = jnp.bfloat16


def iota(shape, axis):
    return lax.broadcasted_iota(jnp.int32, shape, axis)


def row_sums_of(lhs, tile):
    return lax.dot_general(lhs, tile, (((1,), (1,)), ((), ())), preferred_element_type=F32)


def col_sums_of(lhs, tile):
    return lax.dot_general(lhs, tile, (((1,), (0,)), ((), ())), preferred_element_type=F32)


def scatter(by_row, row_at, by_col, col_at):
    out = jnp.zeros((ROWS, TILE), F32)
    rows = iota((ROWS, TILE), 0)
    for j in range(CAP + 1):
        part = jnp.where(row_at == j, by_row, 0.0) + jnp.where(col_at == j, by_col, 0.0)
        out = jnp.where(rows == j, jnp.sum(part, axis=0, keepdims=True), out)
    return out


def gather(window, at):
    out = jnp.zeros((SLOTS, TILE), F32)
    for j in range(CAP + 1):
        out = jnp.where(at == j, window[j : j + 1, :], out)
    return out


def first_kernel(
    c_hbm, count_hbm, row_hbm, col_hbm,
    tiles, sums_ref, spill_ref, first_ref, row_at_ref, col_at_ref, off_at_ref, n_ref,
    count_s, row_s, col_s, tile_sem, int_sem,
):
    ints = [
        pltpu.make_async_copy(count_hbm, count_s, int_sem.at[0]),
        pltpu.make_async_copy(row_hbm, row_s, int_sem.at[1]),
        pltpu.make_async_copy(col_hbm, col_s, int_sem.at[2]),
    ]
    copies = [pltpu.make_async_copy(c_hbm.at[k], tiles.at[k], tile_sem.at[k]) for k in range(SLOTS)]
    for copy in ints:
        copy.start()
    for copy in copies:
        copy.start()
    for copy in ints:
        copy.wait()
    me = lax.axis_index("dev")
    base = me * SLOTS
    count = count_s[me]
    n = (count + 1) // 2
    n_ref[0] = n
    row = [row_s[base + k] for k in range(SLOTS)]
    col = [col_s[base + k] for k in range(SLOTS)]
    start = row[0]
    for k in range(1, SLOTS):
        start = jnp.minimum(start, jnp.where(k < count, row[k], start))
    slots = iota((SLOTS, TILE), 0)
    row_at = jnp.full((SLOTS, TILE), -1, jnp.int32)
    col_at = row_at
    off_at = row_at
    for k in range(SLOTS):
        held = k < count
        local_row = jnp.where(held, row[k] - start, -1)
        local_col = jnp.where(held, col[k] - start, -1)
        local_off = jnp.where(row[k] != col[k], local_col, -1)
        row_at = jnp.where(slots == k, local_row, row_at)
        col_at = jnp.where(slots == k, local_col, col_at)
        off_at = jnp.where(slots == k, local_off, off_at)
    row_at_ref[...] = row_at
    col_at_ref[...] = col_at
    off_at_ref[...] = off_at
    ones = jnp.ones((8, TILE), BF16)
    by_row = jnp.zeros((SLOTS, TILE), F32)
    by_col = by_row
    for k in range(SLOTS):
        copies[k].wait()
        by_row = jnp.where(slots == k, row_sums_of(ones, tiles[k]), by_row)
        by_col = jnp.where(slots == k, col_sums_of(ones, tiles[k]), by_col)
    sums = scatter(by_row, row_at, by_col, off_at)
    sums_ref[...] = sums
    rows = iota((ROWS, TILE), 0)
    first_ref[...] = sums[0:1, :]
    spill_ref[...] = jnp.sum(jnp.where(rows == n, sums, 0.0), axis=0, keepdims=True)


def second_kernel(
    n_ref, tiles, sums_ref, row_at_ref, col_at_ref, off_at_ref, behind_ref, ahead_ref,
    raw_ref, part_ref, scale_ref, spill_ref, first_ref, sent_ref,
):
    n = n_ref[0]
    rows = iota((ROWS, TILE), 0)
    local = sums_ref[...]
    raw = local + jnp.where(rows == 0, behind_ref[...], 0.0) + jnp.where(rows == n, ahead_ref[...], 0.0)
    raw = jnp.where(raw > 0.0, raw, 1.0)
    raw_ref[...] = raw
    own = jnp.where(rows < n, raw, jnp.inf)
    scale = jnp.min(jnp.min(own, axis=0, keepdims=True), axis=1, keepdims=True)
    inverse = scale / raw
    row_at = row_at_ref[...]
    row_inverse = gather(inverse, row_at)
    col_inverse = gather(inverse, col_at_ref[...])
    slots = iota((SLOTS, TILE), 0)

    def halves(x):
        high = x.astype(BF16)
        low = (x - high.astype(F32)).astype(BF16)
        return high, low

    row_high, row_low = halves(row_inverse)
    col_high, col_low = halves(col_inverse)

    def weights(high, low, k):
        return jnp.concatenate(
            [jnp.broadcast_to(high[k : k + 1, :], (8, TILE)), jnp.broadcast_to(low[k : k + 1, :], (8, TILE))], axis=0
        )

    by_row = jnp.zeros((SLOTS, TILE), F32)
    by_col = by_row
    for k in range(SLOTS):
        r = row_sums_of(weights(col_high, col_low, k), tiles[k])
        c = col_sums_of(weights(row_high, row_low, k), tiles[k])
        by_row = jnp.where(slots == k, r[:8] + r[8:], by_row)
        by_col = jnp.where(slots == k, c[:8] + c[8:], by_col)
    part = scatter(by_row * row_inverse, row_at, by_col * col_inverse, off_at_ref[...])
    part_ref[...] = part
    total_one = jnp.sum(jnp.sum(local, axis=0, keepdims=True), axis=1, keepdims=True)
    total_two = jnp.sum(jnp.sum(part, axis=0, keepdims=True), axis=1, keepdims=True)
    sent = jnp.where(iota((1, 128), 1) < 64, total_one, jnp.sqrt(total_two) / scale)
    sent_ref[...] = jnp.broadcast_to(sent, (DEVICES, 128))
    wide = jnp.broadcast_to(scale, (1, 128))
    scale_ref[...] = jnp.broadcast_to(scale, (8, 128))
    first_ref[:, :TILE] = part[0:1, :]
    first_ref[:, TILE:] = wide
    spill_ref[:, :TILE] = jnp.sum(jnp.where(rows == n, part, 0.0), axis=0, keepdims=True)
    spill_ref[:, TILE:] = wide


def factor_kernel(
    n_ref, raw_ref, part_ref, scale_ref, row_at_ref, col_at_ref, behind_ref, ahead_ref,
    weight_ref, row_factor_ref, col_factor_ref,
):
    n = n_ref[0]
    rows = iota((ROWS, TILE), 0)
    scale = jnp.concatenate([scale_ref[0:1, :]] * 4, axis=1)

    def arrived(ref):
        other = jnp.concatenate([ref[:, TILE:]] * 4, axis=1)
        ratio = jnp.where(other > 0.0, scale / jnp.where(other > 0.0, other, 1.0), 0.0)
        return ref[:, :TILE] * ratio * ratio

    part = part_ref[...] + jnp.where(rows == 0, arrived(behind_ref), 0.0) + jnp.where(rows == n, arrived(ahead_ref), 0.0)
    weight = raw_ref[...] / scale * part
    weight = jnp.where(weight > 0.0, weight, 1.0)
    weight_ref[...] = weight
    inverse = 1.0 / weight
    col_factor_ref[...] = gather(inverse, col_at_ref[...])
    upright = jnp.transpose(gather(inverse, row_at_ref[...]))
    for k in range(SLOTS):
        row_factor_ref[k] = jnp.broadcast_to(upright[:, k : k + 1], (TILE, 128))


def last_kernel(
    n_ref, all_ref, c_hbm, raw_ref, weight_ref, scale_ref, row_factor_ref, col_factor_ref,
    one_ref, two_ref, out_hbm, tiles, buffer, in_sem, sem,
):
    copies = [pltpu.make_async_copy(c_hbm.at[k], tiles.at[k], in_sem.at[k]) for k in range(SLOTS)]
    for copy in copies:
        copy.start()
    n = n_ref[0]
    lanes = iota((1, 128), 1)
    everyone = all_ref[...]
    total_one = jnp.sum(everyone, axis=0, keepdims=True)
    mean_one = jnp.sum(jnp.where(lanes == 0, total_one, 0.0), axis=1, keepdims=True) / BINS
    scaled = everyone * mean_one
    total_two = jnp.sum(scaled * scaled, axis=0, keepdims=True)
    mean_two = jnp.sum(jnp.where(lanes == 64, total_two, 0.0), axis=1, keepdims=True) / BINS
    scale = scale_ref[0:1, 0:1]
    unit = scale * mean_two / mean_one
    columns = col_factor_ref[...] * unit * unit * TILE
    for k in range(SLOTS):
        row = jnp.concatenate([row_factor_ref[k]] * 4, axis=1)
        copies[k].wait()
        buffer[k] = (tiles[k].astype(F32) * row * columns[k : k + 1, :]).astype(BF16)
        pltpu.make_async_copy(buffer.at[k], out_hbm.at[k], sem.at[k]).start()
    one = raw_ref[...] / mean_one
    two = weight_ref[...] / unit
    for j in range(CAP):
        one_ref[:, j * TILE : (j + 1) * TILE] = jnp.where(j < n, one[j : j + 1, :], 0.0)
        two_ref[:, j * TILE : (j + 1) * TILE] = jnp.where(j < n, two[j : j + 1, :], 0.0)
    for k in range(SLOTS):
        pltpu.make_async_copy(buffer.at[k], out_hbm.at[k], sem.at[k]).wait()


VMEM = pl.BlockSpec(memory_space=pltpu.VMEM)
SMEM = pl.BlockSpec(memory_space=pltpu.SMEM)
HBM = pl.BlockSpec(memory_space=pltpu.HBM)


def shards(contacts, tile_count, tile_row, tile_col, range_rows):
    forward = [(i, i + 1) for i in range(DEVICES - 1)]
    backward = [(i + 1, i) for i in range(DEVICES - 1)]
    window = pltpu.VMEM((ROWS, TILE), F32)
    index = pltpu.VMEM((SLOTS, TILE), jnp.int32)
    tiles, sums, spill, first, row_at, col_at, off_at, n = pl.pallas_call(
        first_kernel,
        out_shape=(
            pltpu.VMEM((SLOTS, TILE, TILE), BF16), window, pltpu.VMEM((1, TILE), F32), pltpu.VMEM((1, TILE), F32),
            index, index, index, pltpu.SMEM((1,), jnp.int32),
        ),
        in_specs=[HBM] * 4,
        out_specs=(VMEM,) * 7 + (SMEM,),
        scratch_shapes=[
            pltpu.SMEM((DEVICES,), jnp.int32),
            pltpu.SMEM((DEVICES * SLOTS,), jnp.int32),
            pltpu.SMEM((DEVICES * SLOTS,), jnp.int32),
            pltpu.SemaphoreType.DMA((SLOTS,)),
            pltpu.SemaphoreType.DMA((3,)),
        ],
        compiler_params=pltpu.CompilerParams(vmem_limit_bytes=24 << 20),
        name="first",
    )(*(pltpu.with_memory_space_constraint(x, pltpu.HBM) for x in (contacts, tile_count, tile_row, tile_col)))
    behind = lax.ppermute(spill, "dev", forward)
    ahead = lax.ppermute(first, "dev", backward)
    long = pltpu.VMEM((1, TILE + 128), F32)
    raw, part, scale, spill, first, sent = pl.pallas_call(
        second_kernel,
        out_shape=(window, window, pltpu.VMEM((8, 128), F32), long, long, pltpu.VMEM((DEVICES, 128), F32)),
        in_specs=[SMEM] + [VMEM] * 7,
        out_specs=(VMEM,) * 6,
        compiler_params=pltpu.CompilerParams(vmem_limit_bytes=24 << 20),
        name="second",
    )(n, tiles, sums, row_at, col_at, off_at, behind, ahead)
    everyone = lax.all_to_all(sent, "dev", 0, 0, tiled=True)
    behind = lax.ppermute(spill, "dev", forward)
    ahead = lax.ppermute(first, "dev", backward)
    weight, row_factor, col_factor = pl.pallas_call(
        factor_kernel,
        out_shape=(window, pltpu.VMEM((SLOTS, TILE, 128), F32), window),
        in_specs=[SMEM] + [VMEM] * 7,
        out_specs=(VMEM,) * 3,
        compiler_params=pltpu.CompilerParams(vmem_limit_bytes=24 << 20),
        name="factor",
    )(n, raw, part, scale, row_at, col_at, behind, ahead)
    return pl.pallas_call(
        last_kernel,
        out_shape=(
            jax.ShapeDtypeStruct((1, CAP * TILE), F32),
            jax.ShapeDtypeStruct((1, CAP * TILE), F32),
            jax.ShapeDtypeStruct((SLOTS, TILE, TILE), BF16),
        ),
        in_specs=[SMEM, VMEM, HBM] + [VMEM] * 5,
        out_specs=(VMEM, VMEM, HBM),
        scratch_shapes=[pltpu.VMEM((SLOTS, TILE, TILE), BF16)] * 2 + [pltpu.SemaphoreType.DMA((SLOTS,))] * 2,
        compiler_params=pltpu.CompilerParams(vmem_limit_bytes=32 << 20),
        name="last",
    )(n, everyone, pltpu.with_memory_space_constraint(contacts, pltpu.HBM), raw, weight, scale, row_factor, col_factor)


def solution(mesh):
    return jax.shard_map(
        shards,
        mesh=mesh,
        in_specs=(P("dev", None, None), P(), P(), P(), P()),
        out_specs=(P("dev", None), P("dev", None), P("dev", None, None)),
        check_vma=False,
    )
```

time: 103 us -> 49.6 us (0.48)
  other arithmetic: 26.9 us -> 0 us
  starting transfers between devices: 40.4 us -> 28 us
  local copies, waits for them, and re-layouts: 11.2 us -> 0 us
  Pallas kernels: 0 us -> 11.1 us
  waiting for transfers between devices: 19.5 us -> 9.5 us
  between operations: 4.82 us -> 0.7 us
    all_to_all x4 -> x1, waiting for transfers between devices: 17.5 us -> 3.25 us  [shards(): everyone = lax.all_to_all(sent, 'dev', 0, 0, tiled=True)]
    pallas_call x0 -> x4, Pallas kernels: none -> 11.1 us  [the longest x1 3.97 us: shards(): pl.pallas_call(last_kernel, out_shape=(jax.ShapeDtypeStruct((1, CAP * TIL...]
    reduce_sum x8 -> x0, other arithmetic: 11 us -> none  [the longest x2 7.28 us: route_sweep(): col_part = jnp.sum(scaled, 1) * (held_mask * offdiag)[:, None]]
    all_to_all x4 -> x1, starting transfers between devices: 26.8 us -> 16.1 us  [shards(): everyone = lax.all_to_all(sent, 'dev', 0, 0, tiled=True)]
    broadcast_in_dim x4 -> x0, local copies, waits for them, and re-layouts: 5 us -> none  [from_everyone(): jnp.broadcast_to(x[None], (count, *x.shape))]
    convert_element_type x2 -> x0, other arithmetic: 4.97 us -> none  [the longest x1 4.32 us: shards(): (scaled_local(window_b) * TILE * held_mask[:, None, None]).astype(jnp.bfl...]
    ppermute x4, waiting for transfers between devices: 1.98 us -> 6.25 us  [the longest x2 6.24 us: shards(): ahead = lax.ppermute(first, 'dev', backward)]
    select_n x7 -> x0, other arithmetic: 3.46 us -> none  [the longest x1 2.08 us: scaled_local(): inverse[local_col][:, None, :]]
  transfers between devices with their start and end apart: 8 -> 5, of which waited for: 5 -> 3; matrix products, arithmetic and copies ran while one was open for 7% -> 0% of each run, Pallas kernels for 0% -> 2%
where the time goes in v1:
time: 49.6 us; the launch traced here: 49.4 us
  starting transfers between devices  28 us (56%)
  Pallas kernels  11.1 us (22%)
  waiting for transfers between devices  9.5 us (19%)
  between operations  0.7 us (1%)
    all_to_all x1, starting transfers between devices, shards(): everyone = lax.all_to_all(sent, 'dev', 0, 0, tiled=True)  16.1 us
    ppermute x2, starting transfers between devices, shards(): behind = lax.ppermute(spill, 'dev', forward)  8.13 us
    ppermute x2, waiting for transfers between devices, shards(): ahead = lax.ppermute(first, 'dev', backward)  6.24 us
    pallas_call x1, Pallas kernels, shards(): pl.pallas_call(last_kernel, out_shape=(jax.ShapeDtypeStruct((1, CAP * TIL...  3.97 us
    ppermute x2, starting transfers between devices, shards(): ahead = lax.ppermute(first, 'dev', backward)  3.84 us
    pallas_call x1, Pallas kernels, shards(): pl.pallas_call(first_kernel, out_shape=(pltpu.VMEM((SLOTS, TILE, TILE), B...  3.82 us
    all_to_all x1, waiting for transfers between devices, shards(): everyone = lax.all_to_all(sent, 'dev', 0, 0, tiled=True)  3.25 us
    pallas_call x1, Pallas kernels, shards(): pl.pallas_call(second_kernel, out_shape=(window, window, pltpu.VMEM((8, 1...  2.58 us
  transfers between devices with their start and end apart: 5, of which 3 were waited for; matrix products, arithmetic and copies ran while one was open for 0% of the time, Pallas kernels for 2%

profile of v1, /device:TPU:1, one launch (start us, length us, event | category | flops | bytes accessed | tf_op | source)
XLA Modules:
  0.0 49.4 jit_solution(5261506714612120608)
XLA Ops:
  0.6 3.8 %first.1 = (bf16[8,512,512]{2,1,0:T(8,128)(2,1)S(1)}, f32[8,512]{1,0:T(8,128)S(1)}, f32[1,512]{1,0:T(1,128)S(1)}, f32[1,512]{1,0:T(1,128)S(1)}, s32[8,512]{1,0:T...) custom-call(bf16[8,512,512]{2,1,0:T(8,128)(2,1)} %c_hbm.3, s32[256]{0:T(256)} %count_hbm.1, ...), custom_call_target="tpu_custom_call" | custom-call | tf_op jit(solution)/shard_map/first/pallas_call | solution.py:220
  4.5 4.6 %collective-permute-start = (f32[1,512]{1,0:T(1,128)S(1)}, f32[1,512]{1,0:T(1,128)S(1)}, u32[]{:S(2)}, u32[]{:S(2)}) collective-permute-start(f32[1,512]{1,0:T(1,128)S(1)} %get-tuple-element.26), channel_id=1, source_target_pairs={{0,1},{1,2},{2,3},{3,4},{4,5},{5,6},{6,7},{7,8},{8,9},{9,10},{10,1... | collective-permute-start | bytes 6152 | tf_op jit(solution)/shard_map/ppermute | solution.py:238
  9.1 1.9 %collective-permute-start.1 = (f32[1,512]{1,0:T(1,128)S(1)}, f32[1,512]{1,0:T(1,128)S(1)}, u32[]{:S(2)}, u32[]{:S(2)}) collective-permute-start(f32[1,512]{1,0:T(1,128)S(1)} %get-tuple-element.27), channel_id=1, source_target_pairs={{1,0},{2,1},{3,2},{4,3},{5,4},{6,5},{7,6},{8,7},{9,8},{10,9},{11,1... | collective-permute-start | bytes 6152 | tf_op jit(solution)/shard_map/ppermute | solution.py:239
  11.0 0.0 collective-permute-done.behind_ref
  11.0 3.0 %collective-permute-done.1.ahead_ref = f32[1,512]{1,0:T(1,128)S(1)} collective-permute-done((f32[1,512]{1,0:T(1,128)S(1)}, f32[1,512]{1,0:T(1,128)S(1)}, u32[]{:S(2)}, u32[]{:S(2)}) %collective-permute-start.1) | collective-permute-done | bytes 2080 | tf_op jit(solution)/shard_map/ppermute | solution.py:239
  14.0 2.6 %second.1 = (f32[8,512]{1,0:T(8,128)S(1)}, f32[8,512]{1,0:T(8,128)S(1)}, f32[8,128]{1,0:T(8,128)S(1)}, f32[1,640]{1,0:T(1,128)S(1)}, f32[1,640]{1,0:T(1,128)S(1)}, /*index=5*/f32[256,128]{1,0:T(8,128)}) custom-call(s32[1]{0:T(128)S(4)} %get-tuple-element.20.n_ref, bf16[8,512,512]{2,1,0:T(8,128)(2,1)S(1)} %get-tuple-element.21.tiles, ...), custom_call_target="tpu_custom_call" | custom-call | tf_op jit(solution)/shard_map/second/pallas_call | solution.py:241
  16.5 16.1 %all-to-all-start = ((f32[256,1,128]{2,1,0:T(1,128)}), f32[256,1,128]{2,1,0:T(1,128)S(1)}, u32[]{:S(2)}, u32[]{:S(2)}) async-start(f32[256,1,128]{2,1,0:T(1,128)} %bitcast.1), calls=%async_computation | async-start | bytes 262144 | tf_op jit(solution)/shard_map/all_to_all | solution.py:249
  32.6 3.5 %collective-permute-start.2 = (f32[1,640]{1,0:T(1,128)S(1)}, f32[1,640]{1,0:T(1,128)S(1)}, u32[]{:S(2)}, u32[]{:S(2)}) collective-permute-start(f32[1,640]{1,0:T(1,128)S(1)} %get-tuple-element.32), channel_id=1, source_target_pairs={{0,1},{1,2},{2,3},{3,4},{4,5},{5,6},{6,7},{7,8},{8,9},{9,10},{10,1... | collective-permute-start | bytes 7688 | tf_op jit(solution)/shard_map/ppermute | solution.py:250
  36.2 1.9 %collective-permute-start.3 = (f32[1,640]{1,0:T(1,128)S(1)}, f32[1,640]{1,0:T(1,128)S(1)}, u32[]{:S(2)}, u32[]{:S(2)}) collective-permute-start(f32[1,640]{1,0:T(1,128)S(1)} %get-tuple-element.33), channel_id=1, source_target_pairs={{1,0},{2,1},{3,2},{4,3},{5,4},{6,5},{7,6},{8,7},{9,8},{10,9},{11,1... | collective-permute-start | bytes 7688 | tf_op jit(solution)/shard_map/ppermute | solution.py:251
  38.1 0.0 collective-permute-done.2.behind_ref
  38.1 3.3 %collective-permute-done.3.ahead_ref = f32[1,640]{1,0:T(1,128)S(1)} collective-permute-done((f32[1,640]{1,0:T(1,128)S(1)}, f32[1,640]{1,0:T(1,128)S(1)}, u32[]{:S(2)}, u32[]{:S(2)}) %collective-permute-start.3) | collective-permute-done | bytes 2592 | tf_op jit(solution)/shard_map/ppermute | solution.py:251
  41.4 0.8 %factor.1 = (f32[8,512]{1,0:T(8,128)S(1)}, f32[8,512,128]{2,1,0:T(8,128)S(1)}, f32[8,512]{1,0:T(8,128)S(1)}) custom-call(s32[1]{0:T(128)S(4)} %get-tuple-element.20.n_ref, f32[8,512]{1,0:T(8,128)S(1)} %get-tuple-element.29.raw_ref, f32[8,512]{1,0:T(8,128)S(1)} %get-tuple-element.30.part_ref, f32[8,128]{1,0:T(8,128)S(1)} %get-tuple-element.31.scale_ref, ...), custom_call_target="tpu_custom_call" | custom-call | tf_op jit(solution)/shard_map/factor/pallas_call | solution.py:252
  42.1 3.2 %all-to-all-done = f32[256,1,128]{2,1,0:T(1,128)S(1)} async-done(((f32[256,1,128]{2,1,0:T(1,128)}), f32[256,1,128]{2,1,0:T(1,128)S(1)}, u32[]{:S(2)}, u32[]{:S(2)}) %all-to-all-start) | async-done | bytes 131104 | tf_op jit(solution)/shard_map/all_to_all | solution.py:249
  45.4 4.0 %last.1 = (f32[1,2048]{1,0:T(1,128)}, f32[1,2048]{1,0:T(1,128)}, bf16[8,512,512]{2,1,0:T(8,128)(2,1)}) custom-call(s32[1]{0:T(128)S(4)} %get-tuple-element.20.n_ref, f32[256,128]{1,0:T(8,128)S(1)} %bitcast.4, bf16[8,512,512]{2,1,0:T(8,128)(2,1)} %c_hbm.3, f32[8,512]{1,0:T(8,128)S(1)} %get-tuple-element.29.raw_ref, ...), custom_call_target="tpu_custom_call" | custom-call | tf_op jit(solution)/shard_map/last/pallas_call | solution.py:260
Async XLA Ops:
  4.5 6.5 %collective-permute-start = (f32[1,512]{1,0:T(1,128)S(1)}, f32[1,512]{1,0:T(1,128)S(1)}, u32[]{:S(2)}, u32[]{:S(2)}) collective-permute-start(f32[1,512]{1,0:T(1,128)S(1)} %get-tuple-element.26), channel_id=1, source_target_pairs={{0,1},{1,2},{2,3},{3,4},{4,5},{5,6},{6,7},{7,8},{8,9},{9,10},{10,1... | collective-permute-start | bytes 6152 | tf_op jit(solution)/shard_map/ppermute | solution.py:238
  9.1 4.9 %collective-permute-start.1 = (f32[1,512]{1,0:T(1,128)S(1)}, f32[1,512]{1,0:T(1,128)S(1)}, u32[]{:S(2)}, u32[]{:S(2)}) collective-permute-start(f32[1,512]{1,0:T(1,128)S(1)} %get-tuple-element.27), channel_id=1, source_target_pairs={{1,0},{2,1},{3,2},{4,3},{5,4},{6,5},{7,6},{8,7},{9,8},{10,9},{11,1... | collective-permute-start | bytes 6152 | tf_op jit(solution)/shard_map/ppermute | solution.py:239
  16.5 28.8 %all-to-all-start = ((f32[256,1,128]{2,1,0:T(1,128)}), f32[256,1,128]{2,1,0:T(1,128)S(1)}, u32[]{:S(2)}, u32[]{:S(2)}) async-start(f32[256,1,128]{2,1,0:T(1,128)} %bitcast.1), calls=%async_computation | async-start | bytes 262144 | tf_op jit(solution)/shard_map/all_to_all | solution.py:249
  32.6 5.5 %collective-permute-start.2 = (f32[1,640]{1,0:T(1,128)S(1)}, f32[1,640]{1,0:T(1,128)S(1)}, u32[]{:S(2)}, u32[]{:S(2)}) collective-permute-start(f32[1,640]{1,0:T(1,128)S(1)} %get-tuple-element.32), channel_id=1, source_target_pairs={{0,1},{1,2},{2,3},{3,4},{4,5},{5,6},{6,7},{7,8},{8,9},{9,10},{10,1... | collective-permute-start | bytes 7688 | tf_op jit(solution)/shard_map/ppermute | solution.py:250
  36.2 5.2 %collective-permute-start.3 = (f32[1,640]{1,0:T(1,128)S(1)}, f32[1,640]{1,0:T(1,128)S(1)}, u32[]{:S(2)}, u32[]{:S(2)}) collective-permute-start(f32[1,640]{1,0:T(1,128)S(1)} %get-tuple-element.33), channel_id=1, source_target_pairs={{1,0},{2,1},{3,2},{4,3},{5,4},{6,5},{7,6},{8,7},{9,8},{10,9},{11,1... | collective-permute-start | bytes 7688 | tf_op jit(solution)/shard_map/ppermute | solution.py:251

commit v2 on v1

v2 whole, which is shorter than its diff:
```python
import jax
import jax.numpy as jnp
from jax import lax
from jax.experimental import pallas as pl
from jax.experimental.pallas import tpu as pltpu
from jax.sharding import PartitionSpec as P


TILE = 512
SLOTS = 8
ROWS = 8
CAP = 4
EARLY = 4
KEPT = 5
DEVICES = 256
BINS = 262144
F32 = jnp.float32
BF16 = jnp.bfloat16


def iota(shape, axis):
    return lax.broadcasted_iota(jnp.int32, shape, axis)


def row_sums_of(lhs, tile):
    return lax.dot_general(lhs, tile, (((1,), (1,)), ((), ())), preferred_element_type=F32)


def col_sums_of(lhs, tile):
    return lax.dot_general(lhs, tile, (((1,), (0,)), ((), ())), preferred_element_type=F32)


def scatter(by_row, row_at, by_col, col_at):
    out = jnp.zeros((ROWS, TILE), F32)
    rows = iota((ROWS, TILE), 0)
    for j in range(CAP + 1):
        part = jnp.where(row_at == j, by_row, 0.0) + jnp.where(col_at == j, by_col, 0.0)
        out = jnp.where(rows == j, jnp.sum(part, axis=0, keepdims=True), out)
    return out


def gather(window, at):
    out = jnp.zeros((SLOTS, TILE), F32)
    for j in range(CAP + 1):
        out = jnp.where(at == j, window[j : j + 1, :], out)
    return out


def boundary(odd, spill, first):
    return jnp.where(odd, first, spill), jnp.where(odd, spill, first)


def pairs_of(count, off, both, plain):
    for k in range(0, SLOTS, 2):
        usual = jnp.logical_and(off[k] == 0, off[k + 1] != 0)

        @pl.when(jnp.logical_and(k < count, usual))
        def _(k=k):
            plain(k)

        @pl.when(jnp.logical_and(k < count, jnp.logical_not(usual)))
        def _(k=k):
            both(k)


def first_kernel(
    c_hbm, count_hbm, row_hbm, col_hbm,
    tiles, sums_ref, near_ref, far_ref, row_at_ref, col_at_ref, off_at_ref, info_ref,
    count_s, row_s, col_s, by_row_ref, by_col_ref, tile_sem, int_sem,
):
    me = lax.axis_index("dev")
    block = pl.ds(pl.multiple_of((me // 16) * 128, 128), 128)
    ints = [
        pltpu.make_async_copy(count_hbm.at[pl.ds(pl.multiple_of((me // 128) * 128, 128), 128)], count_s, int_sem.at[0]),
        pltpu.make_async_copy(row_hbm.at[block], row_s, int_sem.at[1]),
        pltpu.make_async_copy(col_hbm.at[block], col_s, int_sem.at[2]),
    ]
    copies = [pltpu.make_async_copy(c_hbm.at[k], tiles.at[k], tile_sem.at[k]) for k in range(SLOTS)]
    for copy in ints:
        copy.start()
    for copy in copies[:EARLY]:
        copy.start()
    for copy in ints:
        copy.wait()
    count = count_s[me % 128]
    for k in range(EARLY, SLOTS):

        @pl.when(k - k % 2 < count)
        def _(k=k):
            copies[k].start()

    base = (me % 16) * SLOTS
    n = (count + 1) // 2
    odd = me % 2
    info_ref[0] = n
    info_ref[1] = count
    info_ref[2] = odd
    row = [row_s[base + k] for k in range(SLOTS)]
    col = [col_s[base + k] for k in range(SLOTS)]
    off = [jnp.where(row[k] != col[k], 1, 0) for k in range(SLOTS)]
    off = [jnp.where(k < count, off[k], 1) for k in range(SLOTS)]
    start = row[0]
    for k in range(1, SLOTS):
        start = jnp.minimum(start, jnp.where(k < count, row[k], start))
    slots = iota((SLOTS, TILE), 0)
    row_at = jnp.full((SLOTS, TILE), -1, jnp.int32)
    col_at = row_at
    off_at = row_at
    for k in range(SLOTS):
        info_ref[3 + k] = off[k]
        held = k < count
        local_row = jnp.where(held, row[k] - start, -1)
        local_col = jnp.where(held, col[k] - start, -1)
        local_off = jnp.where(off[k] != 0, local_col, -1)
        row_at = jnp.where(slots == k, local_row, row_at)
        col_at = jnp.where(slots == k, local_col, col_at)
        off_at = jnp.where(slots == k, local_off, off_at)
    row_at_ref[...] = row_at
    col_at_ref[...] = col_at
    off_at_ref[...] = off_at
    ones = jnp.ones((8, TILE), BF16)

    def arrive(k):
        copies[k].wait()
        copies[k + 1].wait()

    def col_of(k):
        total = jnp.sum(tiles[k].astype(F32), axis=0, keepdims=True)
        by_col_ref[k : k + 1, :] = total
        return total

    def plain(k):
        arrive(k)
        by_row_ref[k + 1 : k + 2, :] = row_sums_of(ones, tiles[k + 1])[0:1, :]
        by_row_ref[k : k + 1, :] = col_of(k)
        col_of(k + 1)

    def both(k):
        arrive(k)
        for slot in (k, k + 1):
            by_row_ref[slot : slot + 1, :] = row_sums_of(ones, tiles[slot])[0:1, :]
            col_of(slot)

    pairs_of(count, off, both, plain)
    for k in range(0, EARLY, 2):

        @pl.when(k >= count)
        def _(k=k):
            arrive(k)

    sums = scatter(by_row_ref[...], row_at, by_col_ref[...], off_at)
    sums_ref[...] = sums
    rows = iota((ROWS, TILE), 0)
    spill = jnp.sum(jnp.where(rows == n, sums, 0.0), axis=0, keepdims=True)
    near_ref[...], far_ref[...] = boundary(odd == 1, spill, sums[0:1, :])


def second_kernel(
    info_ref, tiles, sums_ref, row_at_ref, col_at_ref, off_at_ref, near_in, far_in,
    raw_ref, part_ref, scale_ref, near_ref, far_ref, sent_ref,
    by_row_ref, by_col_ref, row_ref, col_ref,
):
    n = info_ref[0]
    count = info_ref[1]
    odd = info_ref[2] == 1
    rows = iota((ROWS, TILE), 0)
    local = sums_ref[...]
    ahead, behind = jnp.where(odd, far_in[...], near_in[...]), jnp.where(odd, near_in[...], far_in[...])
    raw = local + jnp.where(rows == 0, behind, 0.0) + jnp.where(rows == n, ahead, 0.0)
    raw = jnp.where(raw > 0.0, raw, 1.0)
    raw_ref[...] = raw
    own = jnp.where(rows < n, raw, jnp.inf)
    scale = jnp.min(jnp.min(own, axis=0, keepdims=True), axis=1, keepdims=True)
    inverse = scale / raw
    row_at = row_at_ref[...]
    row_inverse = gather(inverse, row_at)
    col_inverse = gather(inverse, col_at_ref[...])
    row_ref[...] = row_inverse
    col_ref[...] = col_inverse

    def weights(ref, k):
        x = jnp.broadcast_to(ref[k : k + 1, :], (8, TILE))
        high = x.astype(BF16)
        low = (x - high.astype(F32)).astype(BF16)
        return jnp.concatenate([high, low], axis=0)

    def row_of(k):
        r = row_sums_of(weights(col_ref, k), tiles[k])
        by_row_ref[k : k + 1, :] = r[0:1, :] + r[8:9, :]

    def col_of(k):
        c = col_sums_of(weights(row_ref, k), tiles[k])
        by_col_ref[k : k + 1, :] = c[0:1, :] + c[8:9, :]

    def plain(k):
        row_of(k + 1)
        row_of(k)
        col_of(k + 1)

    def both(k):
        for slot in (k, k + 1):
            row_of(slot)
            col_of(slot)

    pairs_of(count, [info_ref[3 + k] for k in range(SLOTS)], both, plain)
    part = scatter(by_row_ref[...] * row_inverse, row_at, by_col_ref[...] * col_inverse, off_at_ref[...])
    part_ref[...] = part
    total_one = jnp.sum(jnp.sum(local, axis=0, keepdims=True), axis=1, keepdims=True)
    total_two = jnp.sum(jnp.sum(part, axis=0, keepdims=True), axis=1, keepdims=True)
    sent = jnp.where(iota((1, 128), 1) < 64, total_one, jnp.sqrt(total_two) / scale)
    sent_ref[...] = jnp.broadcast_to(sent, (DEVICES, 128))
    wide = jnp.broadcast_to(scale, (1, 128))
    scale_ref[...] = jnp.broadcast_to(scale, (8, 128))
    spill = jnp.sum(jnp.where(rows == n, part, 0.0), axis=0, keepdims=True)
    near_ref[:, :TILE], far_ref[:, :TILE] = boundary(odd, spill, part[0:1, :])
    near_ref[:, TILE:] = wide
    far_ref[:, TILE:] = wide


def factor_kernel(
    info_ref, c_hbm, raw_ref, part_ref, scale_ref, row_at_ref, col_at_ref, near_in, far_in,
    tiles, weight_ref, row_factor_ref, col_factor_ref, sem,
):
    copy = pltpu.make_async_copy(c_hbm.at[pl.ds(0, KEPT)], tiles, sem)
    copy.start()
    n = info_ref[0]
    odd = info_ref[2] == 1
    rows = iota((ROWS, TILE), 0)
    scale = jnp.concatenate([scale_ref[0:1, :]] * 4, axis=1)
    ahead = jnp.where(odd, far_in[...], near_in[...])
    behind = jnp.where(odd, near_in[...], far_in[...])

    def rescaled(x):
        other = jnp.concatenate([x[:, TILE:]] * 4, axis=1)
        ratio = jnp.where(other > 0.0, scale / jnp.where(other > 0.0, other, 1.0), 0.0)
        return x[:, :TILE] * ratio * ratio

    part = part_ref[...] + jnp.where(rows == 0, rescaled(behind), 0.0) + jnp.where(rows == n, rescaled(ahead), 0.0)
    weight = raw_ref[...] / scale * part
    weight = jnp.where(weight > 0.0, weight, 1.0)
    weight_ref[...] = weight
    inverse = 1.0 / weight
    col_factor_ref[...] = gather(inverse, col_at_ref[...])
    row_factor_ref[...] = jnp.transpose(gather(inverse, row_at_ref[...]))
    copy.wait()


def last_kernel(
    info_ref, all_ref, c_hbm, kept, raw_ref, weight_ref, scale_ref, row_factor_ref, col_factor_ref,
    one_ref, two_ref, out_hbm, tiles, buffer, zeros, columns_ref, in_sem, sem,
):
    n = info_ref[0]
    count = info_ref[1]
    copies = [pltpu.make_async_copy(c_hbm.at[k], tiles.at[k - KEPT], in_sem.at[k - KEPT]) for k in range(KEPT, SLOTS)]
    for k in range(KEPT, SLOTS):

        @pl.when(k < count)
        def _(k=k):
            copies[k - KEPT].start()

    zeros[...] = jnp.zeros((TILE, TILE), BF16)
    for k in range(1, SLOTS):

        @pl.when(k >= count)
        def _(k=k):
            pltpu.make_async_copy(zeros, out_hbm.at[k], sem.at[k]).start()

    lanes = iota((1, 128), 1)
    everyone = all_ref[...]
    total_one = jnp.sum(everyone, axis=0, keepdims=True)
    mean_one = jnp.sum(jnp.where(lanes == 0, total_one, 0.0), axis=1, keepdims=True) / BINS
    scaled = everyone * mean_one
    total_two = jnp.sum(scaled * scaled, axis=0, keepdims=True)
    mean_two = jnp.sum(jnp.where(lanes == 64, total_two, 0.0), axis=1, keepdims=True) / BINS
    scale = scale_ref[0:1, 0:1]
    unit = scale * mean_two / mean_one
    columns_ref[...] = col_factor_ref[...] * unit * unit * TILE
    for k in range(SLOTS):

        @pl.when(k < count)
        def _(k=k):
            if k >= KEPT:
                copies[k - KEPT].wait()
                tile = tiles[k - KEPT]
            else:
                tile = kept[k]
            row = jnp.broadcast_to(row_factor_ref[:, k : k + 1], (TILE, TILE))
            buffer[k] = (tile.astype(F32) * row * columns_ref[k : k + 1, :]).astype(BF16)
            pltpu.make_async_copy(buffer.at[k], out_hbm.at[k], sem.at[k]).start()

    one = raw_ref[...] / mean_one
    two = weight_ref[...] / unit
    for j in range(CAP):
        one_ref[:, j * TILE : (j + 1) * TILE] = jnp.where(j < n, one[j : j + 1, :], 0.0)
        two_ref[:, j * TILE : (j + 1) * TILE] = jnp.where(j < n, two[j : j + 1, :], 0.0)
    for k in range(SLOTS):
        pltpu.make_async_copy(buffer.at[k], out_hbm.at[k], sem.at[k]).wait()


VMEM = pl.BlockSpec(memory_space=pltpu.VMEM)
SMEM = pl.BlockSpec(memory_space=pltpu.SMEM)
HBM = pl.BlockSpec(memory_space=pltpu.HBM)


def in_hbm(x):
    return pltpu.with_memory_space_constraint(x, pltpu.HBM)


def shards(contacts, tile_count, tile_row, tile_col, range_rows):
    near_pairs = [(i, i ^ 1) for i in range(DEVICES)]
    far_pairs = [(i, ((i + 1) ^ 1) - 1) for i in range(1, DEVICES - 1)]
    window = pltpu.VMEM((ROWS, TILE), F32)
    index = pltpu.VMEM((SLOTS, TILE), jnp.int32)
    line = pltpu.VMEM((1, TILE), F32)
    long = pltpu.VMEM((1, TILE + 128), F32)
    tiles, sums, near, far, row_at, col_at, off_at, info = pl.pallas_call(
        first_kernel,
        out_shape=(
            pltpu.VMEM((SLOTS, TILE, TILE), BF16), window, line, line, index, index, index, pltpu.SMEM((11,), jnp.int32),
        ),
        in_specs=[HBM] * 4,
        out_specs=(VMEM,) * 7 + (SMEM,),
        scratch_shapes=[
            pltpu.SMEM((128,), jnp.int32),
            pltpu.SMEM((128,), jnp.int32),
            pltpu.SMEM((128,), jnp.int32),
            window,
            window,
            pltpu.SemaphoreType.DMA((SLOTS,)),
            pltpu.SemaphoreType.DMA((3,)),
        ],
        compiler_params=pltpu.CompilerParams(vmem_limit_bytes=24 << 20),
        name="first",
    )(*(in_hbm(x) for x in (contacts, tile_count, tile_row, tile_col)))
    far = lax.ppermute(far, "dev", far_pairs)
    near = lax.ppermute(near, "dev", near_pairs)
    raw, part, scale, near, far, sent = pl.pallas_call(
        second_kernel,
        out_shape=(window, window, pltpu.VMEM((8, 128), F32), long, long, pltpu.VMEM((DEVICES, 128), F32)),
        in_specs=[SMEM] + [VMEM] * 7,
        out_specs=(VMEM,) * 6,
        scratch_shapes=[window] * 4,
        compiler_params=pltpu.CompilerParams(vmem_limit_bytes=24 << 20),
        name="second",
    )(info, tiles, sums, row_at, col_at, off_at, near, far)
    far = lax.ppermute(far, "dev", far_pairs)
    near = lax.ppermute(near, "dev", near_pairs)
    everyone = lax.all_to_all(sent, "dev", 0, 0, tiled=True)
    tiles, weight, row_factor, col_factor = pl.pallas_call(
        factor_kernel,
        out_shape=(pltpu.VMEM((KEPT, TILE, TILE), BF16), window, pltpu.VMEM((TILE, SLOTS), F32), window),
        in_specs=[SMEM, HBM] + [VMEM] * 7,
        out_specs=(VMEM,) * 4,
        scratch_shapes=[pltpu.SemaphoreType.DMA],
        compiler_params=pltpu.CompilerParams(vmem_limit_bytes=24 << 20),
        name="factor",
    )(info, in_hbm(contacts), raw, part, scale, row_at, col_at, near, far)
    return pl.pallas_call(
        last_kernel,
        out_shape=(
            jax.ShapeDtypeStruct((1, CAP * TILE), F32),
            jax.ShapeDtypeStruct((1, CAP * TILE), F32),
            jax.ShapeDtypeStruct((SLOTS, TILE, TILE), BF16),
        ),
        in_specs=[SMEM, VMEM, HBM] + [VMEM] * 6,
        out_specs=(VMEM, VMEM, HBM),
        scratch_shapes=[
            pltpu.VMEM((SLOTS - KEPT, TILE, TILE), BF16),
            pltpu.VMEM((SLOTS, TILE, TILE), BF16),
            pltpu.VMEM((TILE, TILE), BF16),
            window,
            pltpu.SemaphoreType.DMA((SLOTS - KEPT,)),
            pltpu.SemaphoreType.DMA((SLOTS,)),
        ],
        compiler_params=pltpu.CompilerParams(vmem_limit_bytes=32 << 20),
        name="last",
    )(info, everyone, in_hbm(contacts), tiles, raw, weight, scale, row_factor, col_factor)


def solution(mesh):
    return jax.shard_map(
        shards,
        mesh=mesh,
        in_specs=(P("dev", None, None), P(), P(), P(), P()),
        out_specs=(P("dev", None), P("dev", None), P("dev", None, None)),
        check_vma=False,
    )
```

time: 49.6 us -> 44.3 us (0.89)
  Pallas kernels: 11.1 us -> 7.65 us
  starting transfers between devices: 28 us -> 25.8 us
    pallas_call x1, Pallas kernels: 3.82 us -> 1.67 us  [shards(): pl.pallas_call(first_kernel, out_shape=(pltpu.VMEM((SLOTS, TILE, TILE), B...]
    ppermute x4, starting transfers between devices: 12 us -> 10.3 us  [the longest x2 6.48 us: shards(): near = lax.ppermute(near, 'dev', near_pairs)]
    pallas_call x1, Pallas kernels: 2.58 us -> 1.36 us  [shards(): pl.pallas_call(second_kernel, out_shape=(window, window, pltpu.VMEM((8, 1...]
    pallas_call x1, Pallas kernels: 3.97 us -> 2.87 us  [shards(): pl.pallas_call(last_kernel, out_shape=(jax.ShapeDtypeStruct((1, CAP * TIL...]
    pallas_call x1, Pallas kernels: 0.77 us -> 1.75 us  [shards(): pl.pallas_call(factor_kernel, out_shape=(pltpu.VMEM((KEPT, TILE, TILE), B...]
    all_to_all x1, starting transfers between devices: 16.1 us -> 15.5 us  [shards(): everyone = lax.all_to_all(sent, 'dev', 0, 0, tiled=True)]
  transfers between devices with their start and end apart: 5 -> 5, of which waited for: 3 -> 3; matrix products, arithmetic and copies ran while one was open for 0% -> 0% of each run, Pallas kernels for 2% -> 4%
where the time goes in v2:
time: 44.3 us; the launch traced here: 44 us
  starting transfers between devices  25.8 us (58%)
  waiting for transfers between devices  9.84 us (22%)
  Pallas kernels  7.65 us (17%)
  between operations  0.69 us (2%)
    all_to_all x1, starting transfers between devices, shards(): everyone = lax.all_to_all(sent, 'dev', 0, 0, tiled=True)  15.5 us
    ppermute x2, starting transfers between devices, shards(): near = lax.ppermute(near, 'dev', near_pairs)  6.48 us
    ppermute x2, waiting for transfers between devices, shards(): far = lax.ppermute(far, 'dev', far_pairs)  6.24 us
    ppermute x2, starting transfers between devices, shards(): far = lax.ppermute(far, 'dev', far_pairs)  3.82 us
    all_to_all x1, waiting for transfers between devices, shards(): everyone = lax.all_to_all(sent, 'dev', 0, 0, tiled=True)  3.59 us
    pallas_call x1, Pallas kernels, shards(): pl.pallas_call(last_kernel, out_shape=(jax.ShapeDtypeStruct((1, CAP * TIL...  2.87 us
    pallas_call x1, Pallas kernels, shards(): pl.pallas_call(factor_kernel, out_shape=(pltpu.VMEM((KEPT, TILE, TILE), B...  1.75 us
    pallas_call x1, Pallas kernels, shards(): pl.pallas_call(first_kernel, out_shape=(pltpu.VMEM((SLOTS, TILE, TILE), B...  1.67 us
  transfers between devices with their start and end apart: 5, of which 3 were waited for; matrix products, arithmetic and copies ran while one was open for 0% of the time, Pallas kernels for 4%

profile of v2, /device:TPU:1, one launch (start us, length us, event | category | flops | bytes accessed | tf_op | source)
XLA Modules:
  0.0 44.0 jit_solution(16152355009260395195)
XLA Ops:
  0.6 1.7 %first.1 = (bf16[8,512,512]{2,1,0:T(8,128)(2,1)S(1)}, f32[8,512]{1,0:T(8,128)S(1)}, f32[1,512]{1,0:T(1,128)S(1)}, f32[1,512]{1,0:T(1,128)S(1)}, s32[8,512]{1,0:T...) custom-call(bf16[8,512,512]{2,1,0:T(8,128)(2,1)} %c_hbm.5, s32[256]{0:T(256)} %count_hbm.1, ...), custom_call_target="tpu_custom_call" | custom-call | tf_op jit(solution)/shard_map/first/pallas_call | solution.py:316
  2.3 4.2 %collective-permute-start = (f32[1,512]{1,0:T(1,128)S(1)}, f32[1,512]{1,0:T(1,128)S(1)}, u32[]{:S(2)}, u32[]{:S(2)}) collective-permute-start(f32[1,512]{1,0:T(1,128)S(1)} %get-tuple-element.27), channel_id=1, source_target_pairs={{0,1},{1,0},{2,3},{3,2},{4,5},{5,4},{6,7},{7,6},{8,9},{9,8},{10,11... | collective-permute-start | bytes 6152 | tf_op jit(solution)/shard_map/ppermute | solution.py:336
  6.6 1.9 %collective-permute-start.1 = (f32[1,512]{1,0:T(1,128)S(1)}, f32[1,512]{1,0:T(1,128)S(1)}, u32[]{:S(2)}, u32[]{:S(2)}) collective-permute-start(f32[1,512]{1,0:T(1,128)S(1)} %get-tuple-element.28), channel_id=1, source_target_pairs={{1,2},{2,1},{3,4},{4,3},{5,6},{6,5},{7,8},{8,7},{9,10},{10,9},{11,... | collective-permute-start | bytes 6152 | tf_op jit(solution)/shard_map/ppermute | solution.py:335
  8.5 0.0 collective-permute-done.near_in
  8.5 3.0 %collective-permute-done.1.far_in = f32[1,512]{1,0:T(1,128)S(1)} collective-permute-done((f32[1,512]{1,0:T(1,128)S(1)}, f32[1,512]{1,0:T(1,128)S(1)}, u32[]{:S(2)}, u32[]{:S(2)}) %collective-permute-start.1) | collective-permute-done | bytes 2080 | tf_op jit(solution)/shard_map/ppermute | solution.py:335
  11.5 1.4 %second.1 = (f32[8,512]{1,0:T(8,128)S(1)}, f32[8,512]{1,0:T(8,128)S(1)}, f32[8,128]{1,0:T(8,128)S(1)}, f32[1,640]{1,0:T(1,128)S(1)}, f32[1,640]{1,0:T(1,128)S(1)}, /*index=5*/f32[256,128]{1,0:T(8,128)}) custom-call(s32[11]{0:T(128)S(4)} %get-tuple-element.21.info_ref, bf16[8,512,512]{2,1,0:T(8,128)(2,1)S(1)} %get-tuple-element.22.tiles, ...), custom_call_target="tpu_custom_call" | custom-call | tf_op jit(solution)/shard_map/second/pallas_call | solution.py:337
  12.8 15.5 %all-to-all-start = ((f32[256,1,128]{2,1,0:T(1,128)}), f32[256,1,128]{2,1,0:T(1,128)S(1)}, u32[]{:S(2)}, u32[]{:S(2)}) async-start(f32[256,1,128]{2,1,0:T(1,128)} %bitcast.1), calls=%async_computation | async-start | bytes 262144 | tf_op jit(solution)/shard_map/all_to_all | solution.py:348
  28.4 2.2 %collective-permute-start.2 = (f32[1,640]{1,0:T(1,128)S(1)}, f32[1,640]{1,0:T(1,128)S(1)}, u32[]{:S(2)}, u32[]{:S(2)}) collective-permute-start(f32[1,640]{1,0:T(1,128)S(1)} %get-tuple-element.33), channel_id=1, source_target_pairs={{0,1},{1,0},{2,3},{3,2},{4,5},{5,4},{6,7},{7,6},{8,9},{9,8},{10,11... | collective-permute-start | bytes 7688 | tf_op jit(solution)/shard_map/ppermute | solution.py:347
  30.6 1.9 %collective-permute-start.3 = (f32[1,640]{1,0:T(1,128)S(1)}, f32[1,640]{1,0:T(1,128)S(1)}, u32[]{:S(2)}, u32[]{:S(2)}) collective-permute-start(f32[1,640]{1,0:T(1,128)S(1)} %get-tuple-element.34), channel_id=1, source_target_pairs={{1,2},{2,1},{3,4},{4,3},{5,6},{6,5},{7,8},{8,7},{9,10},{10,9},{11,... | collective-permute-start | bytes 7688 | tf_op jit(solution)/shard_map/ppermute | solution.py:346
  32.5 0.0 collective-permute-done.2.near_in
  32.5 3.3 %collective-permute-done.3.far_in = f32[1,640]{1,0:T(1,128)S(1)} collective-permute-done((f32[1,640]{1,0:T(1,128)S(1)}, f32[1,640]{1,0:T(1,128)S(1)}, u32[]{:S(2)}, u32[]{:S(2)}) %collective-permute-start.3) | collective-permute-done | bytes 2592 | tf_op jit(solution)/shard_map/ppermute | solution.py:346
  35.8 1.7 %factor.1 = (bf16[5,512,512]{2,1,0:T(8,128)(2,1)S(1)}, f32[8,512]{1,0:T(8,128)S(1)}, f32[512,8]{1,0:T(8,128)S(1)}, f32[8,512]{1,0:T(8,128)S(1)}) custom-call(s32[11]{0:T(128)S(4)} %get-tuple-element.21.info_ref, bf16[8,512,512]{2,1,0:T(8,128)(2,1)} %c_hbm.5, f32[8,512]{1,0:T(8,128)S(1)} %get-tuple-element.30.raw_ref, ...), custom_call_target="tpu_custom_call" | custom-call | tf_op jit(solution)/shard_map/factor/pallas_call | solution.py:349
  37.6 3.6 %all-to-all-done = f32[256,1,128]{2,1,0:T(1,128)S(1)} async-done(((f32[256,1,128]{2,1,0:T(1,128)}), f32[256,1,128]{2,1,0:T(1,128)S(1)}, u32[]{:S(2)}, u32[]{:S(2)}) %all-to-all-start) | async-done | bytes 131104 | tf_op jit(solution)/shard_map/all_to_all | solution.py:348
  41.1 2.9 %last.1 = (f32[1,2048]{1,0:T(1,128)}, f32[1,2048]{1,0:T(1,128)}, bf16[8,512,512]{2,1,0:T(8,128)(2,1)}) custom-call(s32[11]{0:T(128)S(4)} %get-tuple-element.21.info_ref, f32[256,128]{1,0:T(8,128)S(1)} %bitcast.4, bf16[8,512,512]{2,1,0:T(8,128)(2,1)} %c_hbm.5, bf16[5,512,512]{2,1,0:T(8,128)(2,1)S(1)} %get-tuple-element.35.kept, ...), custom_call_target="tpu_custom_call" | custom-call | tf_op jit(solution)/shard_map/last/pallas_call | solution.py:358
Async XLA Ops:
  2.3 6.2 %collective-permute-start = (f32[1,512]{1,0:T(1,128)S(1)}, f32[1,512]{1,0:T(1,128)S(1)}, u32[]{:S(2)}, u32[]{:S(2)}) collective-permute-start(f32[1,512]{1,0:T(1,128)S(1)} %get-tuple-element.27), channel_id=1, source_target_pairs={{0,1},{1,0},{2,3},{3,2},{4,5},{5,4},{6,7},{7,6},{8,9},{9,8},{10,11... | collective-permute-start | bytes 6152 | tf_op jit(solution)/shard_map/ppermute | solution.py:336
  6.6 4.9 %collective-permute-start.1 = (f32[1,512]{1,0:T(1,128)S(1)}, f32[1,512]{1,0:T(1,128)S(1)}, u32[]{:S(2)}, u32[]{:S(2)}) collective-permute-start(f32[1,512]{1,0:T(1,128)S(1)} %get-tuple-element.28), channel_id=1, source_target_pairs={{1,2},{2,1},{3,4},{4,3},{5,6},{6,5},{7,8},{8,7},{9,10},{10,9},{11,... | collective-permute-start | bytes 6152 | tf_op jit(solution)/shard_map/ppermute | solution.py:335
  12.8 28.3 %all-to-all-start = ((f32[256,1,128]{2,1,0:T(1,128)}), f32[256,1,128]{2,1,0:T(1,128)S(1)}, u32[]{:S(2)}, u32[]{:S(2)}) async-start(f32[256,1,128]{2,1,0:T(1,128)} %bitcast.1), calls=%async_computation | async-start | bytes 262144 | tf_op jit(solution)/shard_map/all_to_all | solution.py:348
  28.4 4.2 %collective-permute-start.2 = (f32[1,640]{1,0:T(1,128)S(1)}, f32[1,640]{1,0:T(1,128)S(1)}, u32[]{:S(2)}, u32[]{:S(2)}) collective-permute-start(f32[1,640]{1,0:T(1,128)S(1)} %get-tuple-element.33), channel_id=1, source_target_pairs={{0,1},{1,0},{2,3},{3,2},{4,5},{5,4},{6,7},{7,6},{8,9},{9,8},{10,11... | collective-permute-start | bytes 7688 | tf_op jit(solution)/shard_map/ppermute | solution.py:347
  30.6 5.2 %collective-permute-start.3 = (f32[1,640]{1,0:T(1,128)S(1)}, f32[1,640]{1,0:T(1,128)S(1)}, u32[]{:S(2)}, u32[]{:S(2)}) collective-permute-start(f32[1,640]{1,0:T(1,128)S(1)} %get-tuple-element.34), channel_id=1, source_target_pairs={{1,2},{2,1},{3,4},{4,3},{5,6},{6,5},{7,8},{8,7},{9,10},{10,9},{11,... | collective-permute-start | bytes 7688 | tf_op jit(solution)/shard_map/ppermute | solution.py:346

commit v3 on v2

v3 whole, which is shorter than its diff:
```python
import jax
import jax.numpy as jnp
from jax import lax
from jax.experimental import pallas as pl
from jax.experimental.pallas import tpu as pltpu
from jax.sharding import PartitionSpec as P


TILE = 512
SLOTS = 8
ROWS = 8
CAP = 4
EARLY = 4
KEPT = 5
DEVICES = 256
BINS = 262144
AT_ROW, AT_COL, AT_DIAG, AT_OFF, INFO = 3, 11, 19, 23, 27
F32 = jnp.float32
BF16 = jnp.bfloat16


def iota(shape, axis):
    return lax.broadcasted_iota(jnp.int32, shape, axis)


def row_sums_of(lhs, tile):
    return lax.dot_general(lhs, tile, (((1,), (1,)), ((), ())), preferred_element_type=F32)


def col_sums_of(lhs, tile):
    return lax.dot_general(lhs, tile, (((1,), (0,)), ((), ())), preferred_element_type=F32)


def boundary(odd, spill, first):
    return jnp.where(odd, first, spill), jnp.where(odd, spill, first)


def gather(window, at):
    out = jnp.zeros((SLOTS, TILE), F32)
    for j in range(CAP + 1):
        out = jnp.where(at == j, window[j : j + 1, :], out)
    return out


def upright_sum(tile):
    return jnp.sum(tile.astype(F32), axis=0, keepdims=True)


def level_sum(tile):
    return row_sums_of(jnp.ones((8, TILE), BF16), tile)[0:1, :]


def weights(line):
    x = jnp.broadcast_to(line, (8, TILE))
    high = x.astype(BF16)
    low = (x - high.astype(F32)).astype(BF16)
    return jnp.concatenate([high, low], axis=0)


def level(tile, line):
    out = row_sums_of(weights(line), tile)
    return out[0:1, :] + out[8:9, :]


def upright(tile, line):
    out = col_sums_of(weights(line), tile)
    return out[0:1, :] + out[8:9, :]


def edge_kernel(
    c_hbm, count_hbm, row_hbm, col_hbm,
    edge, diagonal, near_ref, far_ref, first_ref, spill_ref, info_ref,
    count_s, row_s, col_s, tile_sem, int_sem,
):
    me = lax.axis_index("dev")
    block = pl.ds(pl.multiple_of((me // 16) * 128, 128), 128)
    ints = [
        pltpu.make_async_copy(count_hbm.at[pl.ds(pl.multiple_of((me // 128) * 128, 128), 128)], count_s, int_sem.at[0]),
        pltpu.make_async_copy(row_hbm.at[block], row_s, int_sem.at[1]),
        pltpu.make_async_copy(col_hbm.at[block], col_s, int_sem.at[2]),
    ]
    copies = [pltpu.make_async_copy(c_hbm.at[max(2 * j - 1, 0)], edge.at[j], tile_sem.at[j]) for j in range(CAP + 1)]
    other = pltpu.make_async_copy(c_hbm.at[2], diagonal, tile_sem.at[CAP + 1])
    for copy in ints:
        copy.start()
    for copy in copies[:EARLY]:
        copy.start()
    other.start()
    for copy in ints:
        copy.wait()
    count = count_s[me % 128]
    for j in range(EARLY, CAP + 1):

        @pl.when(2 * j - 1 < count)
        def _(j=j):
            copies[j].start()

    base = (me % 16) * SLOTS
    n = (count + 1) // 2
    odd = me % 2
    row = [row_s[base + k] for k in range(SLOTS)]
    col = [col_s[base + k] for k in range(SLOTS)]
    start = row[0]
    for k in range(1, SLOTS):
        start = jnp.minimum(start, jnp.where(k < count, row[k], start))
    info_ref[0] = n
    info_ref[1] = count
    info_ref[2] = odd
    for j in range(2 * CAP):
        info_ref[AT_DIAG + j] = 0
    strange = jnp.int32(0)
    for k in range(SLOTS):
        held = k < count
        local_row = jnp.where(held, row[k] - start, -1)
        local_col = jnp.where(held, col[k] - start, -1)
        info_ref[AT_ROW + k] = local_row
        info_ref[AT_COL + k] = local_col
        usual = jnp.logical_and(local_row == k // 2, local_col == (k + 1) // 2)
        strange = jnp.where(jnp.logical_or(usual, jnp.logical_not(held)), strange, 1)

        @pl.when(held)
        def _(k=k, local_row=local_row, local_col=local_col):
            info_ref[jnp.where(local_row == local_col, AT_DIAG, AT_OFF) + local_row] = k

    for copy in copies[:EARLY]:
        copy.wait()
    for j in range(EARLY, CAP + 1):

        @pl.when(2 * j - 1 < count)
        def _(j=j):
            copies[j].wait()

    @pl.when(strange != 0)
    def _():
        for j in range(CAP + 1):
            slot = info_ref[AT_DIAG] if j == 0 else info_ref[AT_OFF + j - 1]
            copy = pltpu.make_async_copy(c_hbm.at[slot], edge.at[j], tile_sem.at[j])
            copy.start()
            copy.wait()

    def rest():
        other.wait()

        @pl.when(strange != 0)
        def _():
            copy = pltpu.make_async_copy(c_hbm.at[info_ref[AT_DIAG + 1]], diagonal, tile_sem.at[CAP + 1])
            copy.start()
            copy.wait()

    first = upright_sum(edge[0]) + jnp.where(count >= 2, level_sum(edge[1]), 0.0)
    spill = jnp.where(count == 2 * n, upright_sum(edge[n]), 0.0)
    first_ref[...] = first
    spill_ref[...] = spill
    near_ref[...], far_ref[...] = boundary(odd == 1, spill, first)
    rest()


def middle_kernel(
    info_ref, c_hbm, edge, one_diagonal, first_ref, spill_ref,
    sums_ref, grown_ref, scale_ref,
    more_diagonals, inverse_ref, sem,
):
    n = info_ref[0]
    count = info_ref[1]
    last = count == 2 * n
    copies = [
        pltpu.make_async_copy(c_hbm.at[info_ref[AT_DIAG + j]], more_diagonals.at[j - 2], sem.at[j - 2])
        for j in range(2, CAP)
    ]
    for j in range(2, CAP):

        @pl.when(j < n)
        def _(j=j):
            copies[j - 2].start()

    def diagonal(j):
        return one_diagonal[...] if j == 1 else more_diagonals[j - 2]

    sums_ref[...] = jnp.zeros((ROWS, TILE), F32)
    grown_ref[...] = jnp.zeros((ROWS, TILE), F32)
    sums_ref[0:1, :] = first_ref[...]
    sums_ref[pl.ds(n, 1), :] = spill_ref[...]
    for j in range(1, CAP):

        @pl.when(j < n)
        def _(j=j):
            above = upright_sum(edge[j])
            across = jnp.where(jnp.logical_or(j + 1 < n, last), level_sum(edge[j + 1]), 0.0)
            if j > 1:
                copies[j - 2].wait()
            sums_ref[j : j + 1, :] = above + across + upright_sum(diagonal(j))

    sums = sums_ref[...]
    rows = iota((ROWS, TILE), 0)
    own = jnp.where(jnp.logical_and(rows < n, sums > 0.0), sums, jnp.inf)
    scale = jnp.min(jnp.min(own, axis=0, keepdims=True), axis=1, keepdims=True)
    total = jnp.sum(jnp.sum(sums, axis=0, keepdims=True), axis=1, keepdims=True)
    scale_ref[...] = jnp.where(iota((8, 128), 0) == 0, scale, total)
    inverse_ref[...] = scale / jnp.where(sums > 0.0, sums, 1.0)
    for j in range(1, CAP):

        @pl.when(j < n)
        def _(j=j):
            line = inverse_ref[j : j + 1, :]
            grown_ref[j - 1 : j, :] += level(edge[j], line)
            grown_ref[j : j + 1, :] += level(diagonal(j), line)
            below = upright(edge[j + 1], line)
            grown_ref[j + 1 : j + 2, :] += jnp.where(jnp.logical_or(j + 1 < n, last), below, 0.0)


def second_kernel(
    info_ref, edge, sums_ref, grown_ref, scale_in, near_in, far_in,
    raw_ref, part_ref, near_ref, far_ref, sent_ref,
    inverse_ref,
):
    n = info_ref[0]
    count = info_ref[1]
    odd = info_ref[2] == 1
    rows = iota((ROWS, TILE), 0)
    local = sums_ref[...]
    ahead, behind = jnp.where(odd, far_in[...], near_in[...]), jnp.where(odd, near_in[...], far_in[...])
    raw = local + jnp.where(rows == 0, behind, 0.0) + jnp.where(rows == n, ahead, 0.0)
    raw = jnp.where(raw > 0.0, raw, 1.0)
    raw_ref[...] = raw
    scale = scale_in[0:1, 0:1]
    inverse = scale / raw
    inverse_ref[...] = inverse
    top = inverse_ref[0:1, :]
    next_row = inverse_ref[pl.ds(n, 1), :]
    here = level(edge[0], top)
    below = jnp.where(count >= 2, upright(edge[1], top), 0.0)
    across = jnp.where(count == 2 * n, level(edge[n], next_row), 0.0)
    grown = grown_ref[...] + jnp.where(rows == 0, here, 0.0) + jnp.where(rows == 1, below, 0.0)
    part = (grown + jnp.where(rows == n - 1, across, 0.0)) * inverse
    part_ref[...] = part
    column = jnp.sum(part, axis=0, keepdims=True)
    quarter = column[:, :128] + column[:, 128:256] + column[:, 256:384] + column[:, 384:]
    folded = jnp.broadcast_to(quarter, (8, 128))
    folded = folded + pltpu.roll(folded, 64, 1)
    sent = jnp.where(iota((8, 128), 1) < 64, scale_in[1:2, :], jnp.sqrt(folded) / scale_in[0:1, :])
    sent_ref[...] = jnp.concatenate([sent] * (DEVICES // 8), axis=0)
    spill = jnp.sum(jnp.where(rows == n, part, 0.0), axis=0, keepdims=True)
    near_ref[:, :TILE], far_ref[:, :TILE] = boundary(odd, spill, part[0:1, :])
    near_ref[:, TILE:] = scale_in[0:1, :]
    far_ref[:, TILE:] = scale_in[0:1, :]


def factor_kernel(
    info_ref, c_hbm, raw_ref, part_ref, scale_ref, near_in, far_in,
    tiles, weight_ref, row_factor_ref, col_factor_ref, out_hbm, zeros, sem, zero_sem,
):
    copy = pltpu.make_async_copy(c_hbm.at[pl.ds(0, KEPT)], tiles, sem)
    copy.start()
    n = info_ref[0]
    count = info_ref[1]
    zeros[...] = jnp.zeros((TILE, TILE), BF16)
    blanks = [None] + [pltpu.make_async_copy(zeros, out_hbm.at[k], zero_sem.at[k]) for k in range(1, SLOTS)]
    for k in range(1, SLOTS):

        @pl.when(k >= count)
        def _(k=k):
            blanks[k].start()

    odd = info_ref[2] == 1
    rows = iota((ROWS, TILE), 0)
    scale = jnp.concatenate([scale_ref[0:1, :]] * 4, axis=1)
    ahead = jnp.where(odd, far_in[...], near_in[...])
    behind = jnp.where(odd, near_in[...], far_in[...])

    def rescaled(x):
        other = jnp.concatenate([x[:, TILE:]] * 4, axis=1)
        ratio = jnp.where(other > 0.0, scale / jnp.where(other > 0.0, other, 1.0), 0.0)
        return x[:, :TILE] * ratio * ratio

    part = part_ref[...] + jnp.where(rows == 0, rescaled(behind), 0.0) + jnp.where(rows == n, rescaled(ahead), 0.0)
    weight = raw_ref[...] / scale * part
    weight = jnp.where(weight > 0.0, weight, 1.0)
    weight_ref[...] = weight
    inverse = 1.0 / weight
    slots = iota((SLOTS, TILE), 0)
    col_at = jnp.full((SLOTS, TILE), -1, jnp.int32)
    for k in range(SLOTS):
        col_at = jnp.where(slots == k, info_ref[AT_COL + k], col_at)
    col_factor_ref[...] = gather(inverse, col_at)
    row_factor_ref[...] = jnp.transpose(inverse)
    copy.wait()
    for k in range(1, SLOTS):

        @pl.when(k >= count)
        def _(k=k):
            blanks[k].wait()


def last_kernel(
    info_ref, all_ref, c_hbm, kept, raw_ref, weight_ref, scale_ref, row_factor_ref, col_factor_ref, blank_hbm,
    one_hbm, two_hbm, out_hbm, tiles, buffer, one_ref, two_ref, columns_ref, rows_ref, in_sem, sem, bias_sem,
):
    n = info_ref[0]
    count = info_ref[1]
    copies = [pltpu.make_async_copy(c_hbm.at[k], tiles.at[k - KEPT], in_sem.at[k - KEPT]) for k in range(KEPT, SLOTS)]
    for k in range(KEPT, SLOTS):

        @pl.when(k < count)
        def _(k=k):
            copies[k - KEPT].start()

    for j in range(CAP):
        rows_ref[j] = jnp.broadcast_to(row_factor_ref[:, j : j + 1], (TILE, 128))
    lanes = iota((1, 128), 1)
    everyone = all_ref[...]
    total_one = jnp.sum(everyone, axis=0, keepdims=True)
    mean_one = jnp.sum(jnp.where(lanes == 0, total_one, 0.0), axis=1, keepdims=True) / BINS
    scaled = everyone * mean_one
    total_two = jnp.sum(scaled * scaled, axis=0, keepdims=True)
    mean_two = jnp.sum(jnp.where(lanes >= 64, total_two, 0.0), axis=1, keepdims=True) / BINS
    scale = scale_ref[0:1, 0:1]
    unit = scale * mean_two / mean_one
    columns_ref[...] = col_factor_ref[...] * unit * unit * TILE
    one = raw_ref[...] / mean_one
    two = weight_ref[...] / unit
    for j in range(CAP):
        one_ref[:, j * TILE : (j + 1) * TILE] = jnp.where(j < n, one[j : j + 1, :], 0.0)
        two_ref[:, j * TILE : (j + 1) * TILE] = jnp.where(j < n, two[j : j + 1, :], 0.0)
    biases = [
        pltpu.make_async_copy(one_ref, one_hbm, bias_sem.at[0]),
        pltpu.make_async_copy(two_ref, two_hbm, bias_sem.at[1]),
    ]
    for copy in biases:
        copy.start()
    for k in range(SLOTS):

        @pl.when(k < count)
        def _(k=k):
            if k >= KEPT:
                copies[k - KEPT].wait()
                tile = tiles[k - KEPT]
            else:
                tile = kept[k]
            row = jnp.concatenate([rows_ref[info_ref[AT_ROW + k]]] * 4, axis=1)
            buffer[k] = (tile.astype(F32) * row * columns_ref[k : k + 1, :]).astype(BF16)
            pltpu.make_async_copy(buffer.at[k], out_hbm.at[k], sem.at[k]).start()

    for copy in biases:
        copy.wait()
    for k in range(SLOTS):

        @pl.when(k < count)
        def _(k=k):
            pltpu.make_async_copy(buffer.at[k], out_hbm.at[k], sem.at[k]).wait()


VMEM = pl.BlockSpec(memory_space=pltpu.VMEM)
SMEM = pl.BlockSpec(memory_space=pltpu.SMEM)
HBM = pl.BlockSpec(memory_space=pltpu.HBM)


def in_hbm(x):
    return pltpu.with_memory_space_constraint(x, pltpu.HBM)


def shards(contacts, tile_count, tile_row, tile_col, range_rows):
    near_pairs = [(i, i ^ 1) for i in range(DEVICES)]
    far_pairs = [(i, ((i + 1) ^ 1) - 1) for i in range(1, DEVICES - 1)]
    window = pltpu.VMEM((ROWS, TILE), F32)
    line = pltpu.VMEM((1, TILE), F32)
    long = pltpu.VMEM((1, TILE + 128), F32)
    splat = pltpu.VMEM((8, 128), F32)
    edge, diagonal, near, far, first, spill, info = pl.pallas_call(
        edge_kernel,
        out_shape=(
            pltpu.VMEM((CAP + 1, TILE, TILE), BF16), pltpu.VMEM((TILE, TILE), BF16), line, line, line, line,
            pltpu.SMEM((INFO,), jnp.int32),
        ),
        in_specs=[HBM] * 4,
        out_specs=(VMEM,) * 6 + (SMEM,),
        scratch_shapes=[
            pltpu.SMEM((128,), jnp.int32),
            pltpu.SMEM((128,), jnp.int32),
            pltpu.SMEM((128,), jnp.int32),
            pltpu.SemaphoreType.DMA((CAP + 2,)),
            pltpu.SemaphoreType.DMA((3,)),
        ],
        compiler_params=pltpu.CompilerParams(vmem_limit_bytes=24 << 20),
        name="edge",
    )(*(in_hbm(x) for x in (contacts, tile_count, tile_row, tile_col)))
    far = lax.ppermute(far, "dev", far_pairs)
    near = lax.ppermute(near, "dev", near_pairs)
    sums, grown, scale = pl.pallas_call(
        middle_kernel,
        out_shape=(window, window, splat),
        in_specs=[SMEM, HBM] + [VMEM] * 4,
        out_specs=(VMEM,) * 3,
        scratch_shapes=[
            pltpu.VMEM((CAP - 2, TILE, TILE), BF16),
            window,
            pltpu.SemaphoreType.DMA((CAP - 2,)),
        ],
        compiler_params=pltpu.CompilerParams(vmem_limit_bytes=24 << 20),
        name="middle",
    )(info, in_hbm(contacts), edge, diagonal, first, spill)
    raw, part, near, far, sent = pl.pallas_call(
        second_kernel,
        out_shape=(window, window, long, long, pltpu.VMEM((DEVICES, 128), F32)),
        in_specs=[SMEM] + [VMEM] * 6,
        out_specs=(VMEM,) * 5,
        scratch_shapes=[window],
        compiler_params=pltpu.CompilerParams(vmem_limit_bytes=24 << 20),
        name="second",
    )(info, edge, sums, grown, scale, near, far)
    far = lax.ppermute(far, "dev", far_pairs)
    near = lax.ppermute(near, "dev", near_pairs)
    everyone = lax.all_to_all(sent, "dev", 0, 0, tiled=True)
    balanced = jax.ShapeDtypeStruct((SLOTS, TILE, TILE), BF16)
    tiles, weight, row_factor, col_factor, blank = pl.pallas_call(
        factor_kernel,
        out_shape=(pltpu.VMEM((KEPT, TILE, TILE), BF16), window, pltpu.VMEM((TILE, SLOTS), F32), window, balanced),
        in_specs=[SMEM, HBM] + [VMEM] * 5,
        out_specs=(VMEM,) * 4 + (HBM,),
        scratch_shapes=[
            pltpu.VMEM((TILE, TILE), BF16), pltpu.SemaphoreType.DMA, pltpu.SemaphoreType.DMA((SLOTS,)),
        ],
        compiler_params=pltpu.CompilerParams(vmem_limit_bytes=24 << 20),
        name="factor",
    )(info, in_hbm(contacts), raw, part, scale, near, far)
    return pl.pallas_call(
        last_kernel,
        out_shape=(
            jax.ShapeDtypeStruct((1, CAP * TILE), F32),
            jax.ShapeDtypeStruct((1, CAP * TILE), F32),
            balanced,
        ),
        in_specs=[SMEM, VMEM, HBM] + [VMEM] * 6 + [HBM],
        out_specs=(HBM,) * 3,
        input_output_aliases={9: 2},
        scratch_shapes=[
            pltpu.VMEM((SLOTS - KEPT, TILE, TILE), BF16),
            pltpu.VMEM((SLOTS, TILE, TILE), BF16),
            pltpu.VMEM((1, CAP * TILE), F32),
            pltpu.VMEM((1, CAP * TILE), F32),
            window,
            pltpu.VMEM((CAP, TILE, 128), F32),
            pltpu.SemaphoreType.DMA((SLOTS - KEPT,)),
            pltpu.SemaphoreType.DMA((SLOTS,)),
            pltpu.SemaphoreType.DMA((2,)),
        ],
        compiler_params=pltpu.CompilerParams(vmem_limit_bytes=32 << 20),
        name="last",
    )(info, everyone, in_hbm(contacts), tiles, raw, weight, scale, row_factor, col_factor, blank)


def solution(mesh):
    return jax.shard_map(
        shards,
        mesh=mesh,
        in_specs=(P("dev", None, None), P(), P(), P(), P()),
        out_specs=(P("dev", None), P("dev", None), P("dev", None, None)),
        check_vma=False,
    )
```

time: 44.3 us -> 42 us (0.948)
  waiting for transfers between devices: 9.84 us -> 8.54 us
  starting transfers between devices: 25.8 us -> 24.6 us
    pallas_call x1, Pallas kernels: 1.75 us -> 2.99 us  [shards(): pl.pallas_call(factor_kernel, out_shape=(pltpu.VMEM((KEPT, TILE, TILE), B...]
    pallas_call x1, Pallas kernels: 2.87 us -> 1.66 us  [shards(): pl.pallas_call(last_kernel, out_shape=(jax.ShapeDtypeStruct((1, CAP * TIL...]
    all_to_all x1, waiting for transfers between devices: 3.59 us -> 2.43 us  [shards(): everyone = lax.all_to_all(sent, 'dev', 0, 0, tiled=True)]
    ppermute x2, starting transfers between devices: 6.48 us -> 5.52 us  [shards(): near = lax.ppermute(near, 'dev', near_pairs)]
    pallas_call x2 -> x3, Pallas kernels: 3.04 us -> 3.25 us  [the longest x1 1.9 us: shards(): pl.pallas_call(edge_kernel, out_shape=(pltpu.VMEM((CAP + 1, TILE, TILE),...]
  transfers between devices with their start and end apart: 5 -> 5, of which waited for: 3 -> 3; matrix products, arithmetic and copies ran while one was open for 0% -> 0% of each run, Pallas kernels for 4% -> 7%
where the time goes in v3:
time: 42 us; the launch traced here: 41.7 us
  starting transfers between devices  24.6 us (59%)
  waiting for transfers between devices  8.54 us (20%)
  Pallas kernels  7.89 us (19%)
  between operations  0.7 us (2%)
    all_to_all x1, starting transfers between devices, shards(): everyone = lax.all_to_all(sent, 'dev', 0, 0, tiled=True)  15.3 us
    ppermute x2, waiting for transfers between devices, shards(): far = lax.ppermute(far, 'dev', far_pairs)  6.1 us
    ppermute x2, starting transfers between devices, shards(): near = lax.ppermute(near, 'dev', near_pairs)  5.52 us
    ppermute x2, starting transfers between devices, shards(): far = lax.ppermute(far, 'dev', far_pairs)  3.82 us
    pallas_call x1, Pallas kernels, shards(): pl.pallas_call(factor_kernel, out_shape=(pltpu.VMEM((KEPT, TILE, TILE), B...  2.99 us
    all_to_all x1, waiting for transfers between devices, shards(): everyone = lax.all_to_all(sent, 'dev', 0, 0, tiled=True)  2.43 us
    pallas_call x1, Pallas kernels, shards(): pl.pallas_call(edge_kernel, out_shape=(pltpu.VMEM((CAP + 1, TILE, TILE),...  1.9 us
    pallas_call x1, Pallas kernels, shards(): pl.pallas_call(last_kernel, out_shape=(jax.ShapeDtypeStruct((1, CAP * TIL...  1.66 us
  transfers between devices with their start and end apart: 5, of which 3 were waited for; matrix products, arithmetic and copies ran while one was open for 0% of the time, Pallas kernels for 7%

profile of v3, /device:TPU:1, one launch (start us, length us, event | category | flops | bytes accessed | tf_op | source)
XLA Modules:
  0.0 41.7 jit_solution(1592204536055265121)
XLA Ops:
  0.6 1.9 %edge.1 = (bf16[5,512,512]{2,1,0:T(8,128)(2,1)S(1)}, bf16[512,512]{1,0:T(8,128)(2,1)S(1)}, f32[1,512]{1,0:T(1,128)S(1)}, f32[1,512]{1,0:T(1,128)S(1)}, f32[1,512...) custom-call(bf16[8,512,512]{2,1,0:T(8,128)(2,1)} %c_hbm.7, s32[256]{0:T(256)} %count_hbm.1, s32[2048]{0:T(1024)} %row_hbm.1, ...), custom_call_target="tpu_custom_call" | custom-call | tf_op jit(solution)/shard_map/edge/pallas_call | solution.py:368
  2.5 3.3 %collective-permute-start = (f32[1,512]{1,0:T(1,128)S(1)}, f32[1,512]{1,0:T(1,128)S(1)}, u32[]{:S(2)}, u32[]{:S(2)}) collective-permute-start(f32[1,512]{1,0:T(1,128)S(1)} %get-tuple-element.31), channel_id=1, source_target_pairs={{0,1},{1,0},{2,3},{3,2},{4,5},{5,4},{6,7},{7,6},{8,9},{9,8},{10,11... | collective-permute-start | bytes 6152 | tf_op jit(solution)/shard_map/ppermute | solution.py:387
  5.8 1.9 %collective-permute-start.1 = (f32[1,512]{1,0:T(1,128)S(1)}, f32[1,512]{1,0:T(1,128)S(1)}, u32[]{:S(2)}, u32[]{:S(2)}) collective-permute-start(f32[1,512]{1,0:T(1,128)S(1)} %get-tuple-element.32), channel_id=1, source_target_pairs={{1,2},{2,1},{3,4},{4,3},{5,6},{6,5},{7,8},{8,7},{9,10},{10,9},{11,... | collective-permute-start | bytes 6152 | tf_op jit(solution)/shard_map/ppermute | solution.py:386
  7.7 0.1 middle.1
  7.9 0.0 collective-permute-done.near_in
  7.9 2.8 %collective-permute-done.1.far_in = f32[1,512]{1,0:T(1,128)S(1)} collective-permute-done((f32[1,512]{1,0:T(1,128)S(1)}, f32[1,512]{1,0:T(1,128)S(1)}, u32[]{:S(2)}, u32[]{:S(2)}) %collective-permute-start.1) | collective-permute-done | bytes 2080 | tf_op jit(solution)/shard_map/ppermute | solution.py:386
  10.7 1.2 %second.1 = (f32[8,512]{1,0:T(8,128)S(1)}, f32[8,512]{1,0:T(8,128)S(1)}, f32[1,640]{1,0:T(1,128)S(1)}, f32[1,640]{1,0:T(1,128)S(1)}, f32[256,128]{1,0:T(8,128)}) custom-call(s32[27]{0:T(128)S(4)} %get-tuple-element.23.info_ref, bf16[5,512,512]{2,1,0:T(8,128)(2,1)S(1)} %get-tuple-element.24.edge, f32[8,512]{1,0:T(8,128)S(1)} %get-tuple-element.28.sums_ref, ...), custom_call_target="tpu_custom_call" | custom-call | tf_op jit(solution)/shard_map/second/pallas_call | solution.py:401
  11.9 15.3 %all-to-all-start = ((f32[256,1,128]{2,1,0:T(1,128)}), f32[256,1,128]{2,1,0:T(1,128)S(1)}, u32[]{:S(2)}, u32[]{:S(2)}) async-start(f32[256,1,128]{2,1,0:T(1,128)} %bitcast.1), calls=%async_computation | async-start | bytes 262144 | tf_op jit(solution)/shard_map/all_to_all | solution.py:412
  27.2 2.2 %collective-permute-start.2 = (f32[1,640]{1,0:T(1,128)S(1)}, f32[1,640]{1,0:T(1,128)S(1)}, u32[]{:S(2)}, u32[]{:S(2)}) collective-permute-start(f32[1,640]{1,0:T(1,128)S(1)} %get-tuple-element.36), channel_id=1, source_target_pairs={{0,1},{1,0},{2,3},{3,2},{4,5},{5,4},{6,7},{7,6},{8,9},{9,8},{10,11... | collective-permute-start | bytes 7688 | tf_op jit(solution)/shard_map/ppermute | solution.py:411
  29.4 1.9 %collective-permute-start.3 = (f32[1,640]{1,0:T(1,128)S(1)}, f32[1,640]{1,0:T(1,128)S(1)}, u32[]{:S(2)}, u32[]{:S(2)}) collective-permute-start(f32[1,640]{1,0:T(1,128)S(1)} %get-tuple-element.37), channel_id=1, source_target_pairs={{1,2},{2,1},{3,4},{4,3},{5,6},{6,5},{7,8},{8,7},{9,10},{10,9},{11,... | collective-permute-start | bytes 7688 | tf_op jit(solution)/shard_map/ppermute | solution.py:410
  31.4 0.0 collective-permute-done.2.near_in
  31.4 3.3 %collective-permute-done.3.far_in = f32[1,640]{1,0:T(1,128)S(1)} collective-permute-done((f32[1,640]{1,0:T(1,128)S(1)}, f32[1,640]{1,0:T(1,128)S(1)}, u32[]{:S(2)}, u32[]{:S(2)}) %collective-permute-start.3) | collective-permute-done | bytes 2592 | tf_op jit(solution)/shard_map/ppermute | solution.py:410
  34.6 3.0 %factor.1 = (bf16[5,512,512]{2,1,0:T(8,128)(2,1)S(1)}, f32[8,512]{1,0:T(8,128)S(1)}, f32[512,8]{1,0:T(8,128)S(1)}, f32[8,512]{1,0:T(8,128)S(1)}, bf16[8,512,512]{2,1,0:T(8,128)(2,1)}) custom-call(s32[27]{0:T(128)S(4)} %get-tuple-element.23.info_ref, bf16[8,512,512]{2,1,0:T(8,128)(2,1)} %c_hbm.7, f32[8,512]{1,0:T(8,128)S(1)} %get-tuple-element.34.raw_ref, ...), custom_call_target="tpu_custom_call" | custom-call | tf_op jit(solution)/shard_map/factor/pallas_call | solution.py:414
  37.6 2.4 %all-to-all-done = f32[256,1,128]{2,1,0:T(1,128)S(1)} async-done(((f32[256,1,128]{2,1,0:T(1,128)}), f32[256,1,128]{2,1,0:T(1,128)S(1)}, u32[]{:S(2)}, u32[]{:S(2)}) %all-to-all-start) | async-done | bytes 131104 | tf_op jit(solution)/shard_map/all_to_all | solution.py:412
  40.1 1.7 %last.1 = (f32[1,2048]{1,0:T(1,128)}, f32[1,2048]{1,0:T(1,128)}, bf16[8,512,512]{2,1,0:T(8,128)(2,1)}) custom-call(s32[27]{0:T(128)S(4)} %get-tuple-element.23.info_ref, f32[256,128]{1,0:T(8,128)S(1)} %bitcast.4, bf16[8,512,512]{2,1,0:T(8,128)(2,1)} %c_hbm.7, bf16[5,512,512]{2,1,0:T(8,128)(2,1)S(1)} %get-tuple-element.38.kept, ...), custom_call_target="tpu_custom_call", output_to_operand_aliasing={{2}: (9, {})} | custom-call | tf_op jit(solution)/shard_map/last/pallas_call | solution.py:425
Async XLA Ops:
  2.5 5.3 %collective-permute-start = (f32[1,512]{1,0:T(1,128)S(1)}, f32[1,512]{1,0:T(1,128)S(1)}, u32[]{:S(2)}, u32[]{:S(2)}) collective-permute-start(f32[1,512]{1,0:T(1,128)S(1)} %get-tuple-element.31), channel_id=1, source_target_pairs={{0,1},{1,0},{2,3},{3,2},{4,5},{5,4},{6,7},{7,6},{8,9},{9,8},{10,11... | collective-permute-start | bytes 6152 | tf_op jit(solution)/shard_map/ppermute | solution.py:387
  5.8 4.9 %collective-permute-start.1 = (f32[1,512]{1,0:T(1,128)S(1)}, f32[1,512]{1,0:T(1,128)S(1)}, u32[]{:S(2)}, u32[]{:S(2)}) collective-permute-start(f32[1,512]{1,0:T(1,128)S(1)} %get-tuple-element.32), channel_id=1, source_target_pairs={{1,2},{2,1},{3,4},{4,3},{5,6},{6,5},{7,8},{8,7},{9,10},{10,9},{11,... | collective-permute-start | bytes 6152 | tf_op jit(solution)/shard_map/ppermute | solution.py:386
  11.9 28.1 %all-to-all-start = ((f32[256,1,128]{2,1,0:T(1,128)}), f32[256,1,128]{2,1,0:T(1,128)S(1)}, u32[]{:S(2)}, u32[]{:S(2)}) async-start(f32[256,1,128]{2,1,0:T(1,128)} %bitcast.1), calls=%async_computation | async-start | bytes 262144 | tf_op jit(solution)/shard_map/all_to_all | solution.py:412
  27.2 4.2 %collective-permute-start.2 = (f32[1,640]{1,0:T(1,128)S(1)}, f32[1,640]{1,0:T(1,128)S(1)}, u32[]{:S(2)}, u32[]{:S(2)}) collective-permute-start(f32[1,640]{1,0:T(1,128)S(1)} %get-tuple-element.36), channel_id=1, source_target_pairs={{0,1},{1,0},{2,3},{3,2},{4,5},{5,4},{6,7},{7,6},{8,9},{9,8},{10,11... | collective-permute-start | bytes 7688 | tf_op jit(solution)/shard_map/ppermute | solution.py:411
  29.4 5.2 %collective-permute-start.3 = (f32[1,640]{1,0:T(1,128)S(1)}, f32[1,640]{1,0:T(1,128)S(1)}, u32[]{:S(2)}, u32[]{:S(2)}) collective-permute-start(f32[1,640]{1,0:T(1,128)S(1)} %get-tuple-element.37), channel_id=1, source_target_pairs={{1,2},{2,1},{3,4},{4,3},{5,6},{6,5},{7,8},{8,7},{9,10},{10,9},{11,... | collective-permute-start | bytes 7688 | tf_op jit(solution)/shard_map/ppermute | solution.py:410

commit v4 on v3

--- a/solution.py
+++ b/solution.py
@@ -11,10 +11,11 @@
 ROWS = 8
 CAP = 4
 EARLY = 4
+HALVES = 1
 KEPT = 5
 DEVICES = 256
 BINS = 262144
-AT_ROW, AT_COL, AT_DIAG, AT_OFF, INFO = 3, 11, 19, 23, 27
+AT_ROW, AT_COL, AT_DIAG, AT_OFF, EARLY_BIRD, STRANGE, INFO = 3, 11, 19, 23, 27, 28, 29
 F32 = jnp.float32
 BF16 = jnp.bfloat16
 
@@ -67,10 +68,59 @@
     return out[0:1, :] + out[8:9, :]
 
 
+def interior(
+    info_ref, c_hbm, edge, diagonals, first_ref, spill_ref,
+    sums_ref, grown_ref, scale_ref,
+    last_diagonal, inverse_ref, sem,
+):
+    n = info_ref[0]
+    count = info_ref[1]
+    last = count == 2 * n
+    copy = pltpu.make_async_copy(c_hbm.at[info_ref[AT_DIAG + CAP - 1]], last_diagonal, sem)
+
+    @pl.when(n == CAP)
+    def _():
+        copy.start()
+
+    def diagonal(j):
+        return last_diagonal[...] if j == CAP - 1 else diagonals[j - 1]
+
+    sums_ref[...] = jnp.zeros((ROWS, TILE), F32)
+    grown_ref[...] = jnp.zeros((ROWS, TILE), F32)
+    sums_ref[0:1, :] = first_ref[...]
+    sums_ref[pl.ds(n, 1), :] = spill_ref[...]
+    for j in range(1, CAP):
+
+        @pl.when(j < n)
+        def _(j=j):
+            above = upright_sum(edge[j])
+            across = jnp.where(jnp.logical_or(j + 1 < n, last), level_sum(edge[j + 1]), 0.0)
+            if j == CAP - 1:
+                copy.wait()
+            sums_ref[j : j + 1, :] = above + across + upright_sum(diagonal(j))
+
+    sums = sums_ref[...]
+    rows = iota((ROWS, TILE), 0)
+    own = jnp.where(jnp.logical_and(rows < n, sums > 0.0), sums, jnp.inf)
+    scale = jnp.min(jnp.min(own, axis=0, keepdims=True), axis=1, keepdims=True)
+    total = jnp.sum(jnp.sum(sums, axis=0, keepdims=True), axis=1, keepdims=True)
+    scale_ref[...] = jnp.where(iota((8, 128), 0) == 0, scale, total)
+    inverse_ref[...] = scale / jnp.where(sums > 0.0, sums, 1.0)
+    for j in range(1, CAP):
+
+        @pl.when(j < n)
+        def _(j=j):
+            line = inverse_ref[j : j + 1, :]
+            grown_ref[j - 1 : j, :] += level(edge[j], line)
+            grown_ref[j : j + 1, :] += level(diagonal(j), line)
+            below = upright(edge[j + 1], line)
+            grown_ref[j + 1 : j + 2, :] += jnp.where(jnp.logical_or(j + 1 < n, last), below, 0.0)
+
+
 def edge_kernel(
     c_hbm, count_hbm, row_hbm, col_hbm,
-    edge, diagonal, near_ref, far_ref, first_ref, spill_ref, info_ref,
-    count_s, row_s, col_s, tile_sem, int_sem,
+    edge, diagonal, near_ref, far_ref, first_ref, spill_ref, sums_ref, grown_ref, scale_ref, info_ref,
+    count_s, row_s, col_s, last_diagonal, inverse_ref, tile_sem, int_sem, sem,
 ):
     me = lax.axis_index("dev")
     block = pl.ds(pl.multiple_of((me // 16) * 128, 128), 128)
@@ -80,23 +130,29 @@
         pltpu.make_async_copy(col_hbm.at[block], col_s, int_sem.at[2]),
     ]
     copies = [pltpu.make_async_copy(c_hbm.at[max(2 * j - 1, 0)], edge.at[j], tile_sem.at[j]) for j in range(CAP + 1)]
-    other = pltpu.make_async_copy(c_hbm.at[2], diagonal, tile_sem.at[CAP + 1])
+    others = [
+        pltpu.make_async_copy(c_hbm.at[2 * j], diagonal.at[j - 1], tile_sem.at[CAP + j]) for j in (1, 2)
+    ]
     for copy in ints:
         copy.start()
     for copy in copies[:EARLY]:
         copy.start()
-    other.start()
+    others[0].start()
     for copy in ints:
         copy.wait()
     count = count_s[me % 128]
+    n = (count + 1) // 2
     for j in range(EARLY, CAP + 1):
 
         @pl.when(2 * j - 1 < count)
         def _(j=j):
             copies[j].start()
 
+    @pl.when(n > 2)
+    def _():
+        others[1].start()
+
     base = (me % 16) * SLOTS
-    n = (count + 1) // 2
     odd = me % 2
     row = [row_s[base + k] for k in range(SLOTS)]
     col = [col_s[base + k] for k in range(SLOTS)]
@@ -122,13 +178,49 @@
         def _(k=k, local_row=local_row, local_col=local_col):
             info_ref[jnp.where(local_row == local_col, AT_DIAG, AT_OFF) + local_row] = k
 
-    for copy in copies[:EARLY]:
-        copy.wait()
-    for j in range(EARLY, CAP + 1):
-
-        @pl.when(2 * j - 1 < count)
+    info_ref[STRANGE] = strange
+
+    def rest():
+        for j in range(2, EARLY):
+
+            @pl.when(j > n)
+            def _(j=j):
+                copies[j].wait()
+
+        others[0].wait()
+
+        @pl.when(n > 2)
+        def _():
+            others[1].wait()
+
+        @pl.when(strange != 0)
+        def _():
+            for j in (1, 2):
+                copy = pltpu.make_async_copy(
+                    c_hbm.at[info_ref[AT_DIAG + j]], diagonal.at[j - 1], tile_sem.at[CAP + j]
+                )
+                copy.start()
+                copy.wait()
+
+    def first_of(part):
+        return part + jnp.where(count >= 2, level_sum(edge[1]), 0.0)
+
+    def spill_of():
+        return jnp.where(count == 2 * n, upright_sum(edge[n]), 0.0)
+
+    copies[0].wait()
+    copies[1].wait()
+    first_ref[...] = first_of(upright_sum(edge[0]))
+    for j in range(2, CAP + 1):
+
+        @pl.when(j <= n)
         def _(j=j):
-            copies[j].wait()
+            if j >= EARLY:
+                pl.when(2 * j - 1 < count)(copies[j].wait)
+            else:
+                copies[j].wait()
+
+    spill_ref[...] = spill_of()
 
     @pl.when(strange != 0)
     def _():
@@ -137,75 +229,33 @@
             copy = pltpu.make_async_copy(c_hbm.at[slot], edge.at[j], tile_sem.at[j])
             copy.start()
             copy.wait()
-
-    def rest():
-        other.wait()
-
-        @pl.when(strange != 0)
-        def _():
-            copy = pltpu.make_async_copy(c_hbm.at[info_ref[AT_DIAG + 1]], diagonal, tile_sem.at[CAP + 1])
-            copy.start()
-            copy.wait()
-
-    first = upright_sum(edge[0]) + jnp.where(count >= 2, level_sum(edge[1]), 0.0)
-    spill = jnp.where(count == 2 * n, upright_sum(edge[n]), 0.0)
-    first_ref[...] = first
-    spill_ref[...] = spill
-    near_ref[...], far_ref[...] = boundary(odd == 1, spill, first)
+        first_ref[...] = first_of(upright_sum(edge[0]))
+        spill_ref[...] = spill_of()
+
+    near_ref[...], far_ref[...] = boundary(odd == 1, spill_ref[...], first_ref[...])
     rest()
+    ahead_of_partner = jnp.logical_or(jnp.logical_and(odd == 1, me % 8 != 7), jnp.logical_and(me % 64 == 0, me > 0))
+    info_ref[EARLY_BIRD] = jnp.where(ahead_of_partner, 1, 0)
+
+    @pl.when(ahead_of_partner)
+    def _():
+        interior(
+            info_ref, c_hbm, edge, diagonal, first_ref, spill_ref, sums_ref, grown_ref, scale_ref,
+            last_diagonal, inverse_ref, sem,
+        )
 
 
 def middle_kernel(
-    info_ref, c_hbm, edge, one_diagonal, first_ref, spill_ref,
+    info_ref, c_hbm, edge, diagonals, first_ref, spill_ref, sums_in, grown_in, scale_in,
     sums_ref, grown_ref, scale_ref,
-    more_diagonals, inverse_ref, sem,
+    last_diagonal, inverse_ref, sem,
 ):
-    n = info_ref[0]
-    count = info_ref[1]
-    last = count == 2 * n
-    copies = [
-        pltpu.make_async_copy(c_hbm.at[info_ref[AT_DIAG + j]], more_diagonals.at[j - 2], sem.at[j - 2])
-        for j in range(2, CAP)
-    ]
-    for j in range(2, CAP):
-
-        @pl.when(j < n)
-        def _(j=j):
-            copies[j - 2].start()
-
-    def diagonal(j):
-        return one_diagonal[...] if j == 1 else more_diagonals[j - 2]
-
-    sums_ref[...] = jnp.zeros((ROWS, TILE), F32)
-    grown_ref[...] = jnp.zeros((ROWS, TILE), F32)
-    sums_ref[0:1, :] = first_ref[...]
-    sums_ref[pl.ds(n, 1), :] = spill_ref[...]
-    for j in range(1, CAP):
-
-        @pl.when(j < n)
-        def _(j=j):
-            above = upright_sum(edge[j])
-            across = jnp.where(jnp.logical_or(j + 1 < n, last), level_sum(edge[j + 1]), 0.0)
-            if j > 1:
-                copies[j - 2].wait()
-            sums_ref[j : j + 1, :] = above + across + upright_sum(diagonal(j))
-
-    sums = sums_ref[...]
-    rows = iota((ROWS, TILE), 0)
-    own = jnp.where(jnp.logical_and(rows < n, sums > 0.0), sums, jnp.inf)
-    scale = jnp.min(jnp.min(own, axis=0, keepdims=True), axis=1, keepdims=True)
-    total = jnp.sum(jnp.sum(sums, axis=0, keepdims=True), axis=1, keepdims=True)
-    scale_ref[...] = jnp.where(iota((8, 128), 0) == 0, scale, total)
-    inverse_ref[...] = scale / jnp.where(sums > 0.0, sums, 1.0)
-    for j in range(1, CAP):
-
-        @pl.when(j < n)
-        def _(j=j):
-            line = inverse_ref[j : j + 1, :]
-            grown_ref[j - 1 : j, :] += level(edge[j], line)
-            grown_ref[j : j + 1, :] += level(diagonal(j), line)
-            below = upright(edge[j + 1], line)
-            grown_ref[j + 1 : j + 2, :] += jnp.where(jnp.logical_or(j + 1 < n, last), below, 0.0)
+    @pl.when(info_ref[EARLY_BIRD] == 0)
+    def _():
+        interior(
+            info_ref, c_hbm, edge, diagonals, first_ref, spill_ref, sums_ref, grown_ref, scale_ref,
+            last_diagonal, inverse_ref, sem,
+        )
 
 
 def second_kernel(
@@ -304,17 +354,29 @@
         def _(k=k):
             copies[k - KEPT].start()
 
-    for j in range(CAP):
+
+    def send(k, half):
+        part = pl.ds(half * TILE // HALVES, TILE // HALVES)
+        return pltpu.make_async_copy(buffer.at[k, part], out_hbm.at[k, part], sem.at[k, half])
+
+    def broadcast_row(j):
         rows_ref[j] = jnp.broadcast_to(row_factor_ref[:, j : j + 1], (TILE, 128))
+
+    @pl.when(info_ref[STRANGE] != 0)
+    def _():
+        for j in range(1, CAP):
+            broadcast_row(j)
+
+    broadcast_row(0)
     lanes = iota((1, 128), 1)
     everyone = all_ref[...]
+    scale = scale_ref[0:1, 0:1]
+    scaled = everyone * scale_ref[0:1, :]
     total_one = jnp.sum(everyone, axis=0, keepdims=True)
+    total_two = jnp.sum(scaled * scaled, axis=0, keepdims=True)
     mean_one = jnp.sum(jnp.where(lanes == 0, total_one, 0.0), axis=1, keepdims=True) / BINS
-    scaled = everyone * mean_one
-    total_two = jnp.sum(scaled * scaled, axis=0, keepdims=True)
-    mean_two = jnp.sum(jnp.where(lanes >= 64, total_two, 0.0), axis=1, keepdims=True) / BINS
-    scale = scale_ref[0:1, 0:1]
-    unit = scale * mean_two / mean_one
+    sum_two = jnp.sum(jnp.where(lanes >= 64, total_two, 0.0), axis=1, keepdims=True)
+    unit = (sum_two / BINS) * (mean_one / scale)
     columns_ref[...] = col_factor_ref[...] * unit * unit * TILE
     one = raw_ref[...] / mean_one
     two = weight_ref[...] / unit
@@ -331,14 +393,19 @@
 
         @pl.when(k < count)
         def _(k=k):
+            if k > 0 and k % 2 == 0:
+                broadcast_row(k // 2)
             if k >= KEPT:
                 copies[k - KEPT].wait()
                 tile = tiles[k - KEPT]
             else:
                 tile = kept[k]
             row = jnp.concatenate([rows_ref[info_ref[AT_ROW + k]]] * 4, axis=1)
-            buffer[k] = (tile.astype(F32) * row * columns_ref[k : k + 1, :]).astype(BF16)
-            pltpu.make_async_copy(buffer.at[k], out_hbm.at[k], sem.at[k]).start()
+            columns = columns_ref[k : k + 1, :]
+            for half in range(HALVES):
+                part = slice(half * TILE // HALVES, (half + 1) * TILE // HALVES)
+                buffer[k, part] = (tile[part].astype(F32) * row[part] * columns).astype(BF16)
+                send(k, half).start()
 
     for copy in biases:
         copy.wait()
@@ -346,7 +413,8 @@
 
         @pl.when(k < count)
         def _(k=k):
-            pltpu.make_async_copy(buffer.at[k], out_hbm.at[k], sem.at[k]).wait()
+            for half in range(HALVES):
+                send(k, half).wait()
 
 
 VMEM = pl.BlockSpec(memory_space=pltpu.VMEM)
@@ -365,20 +433,23 @@
     line = pltpu.VMEM((1, TILE), F32)
     long = pltpu.VMEM((1, TILE + 128), F32)
     splat = pltpu.VMEM((8, 128), F32)
-    edge, diagonal, near, far, first, spill, info = pl.pallas_call(
+    edge, diagonal, near, far, first, spill, sums, grown, scale, info = pl.pallas_call(
         edge_kernel,
         out_shape=(
-            pltpu.VMEM((CAP + 1, TILE, TILE), BF16), pltpu.VMEM((TILE, TILE), BF16), line, line, line, line,
-            pltpu.SMEM((INFO,), jnp.int32),
+            pltpu.VMEM((CAP + 1, TILE, TILE), BF16), pltpu.VMEM((2, TILE, TILE), BF16), line, line, line, line,
+            window, window, splat, pltpu.SMEM((INFO,), jnp.int32),
         ),
         in_specs=[HBM] * 4,
-        out_specs=(VMEM,) * 6 + (SMEM,),
+        out_specs=(VMEM,) * 9 + (SMEM,),
         scratch_shapes=[
             pltpu.SMEM((128,), jnp.int32),
             pltpu.SMEM((128,), jnp.int32),
             pltpu.SMEM((128,), jnp.int32),
-            pltpu.SemaphoreType.DMA((CAP + 2,)),
+            pltpu.VMEM((TILE, TILE), BF16),
+            window,
+            pltpu.SemaphoreType.DMA((CAP + 3,)),
             pltpu.SemaphoreType.DMA((3,)),
+            pltpu.SemaphoreType.DMA,
         ],
         compiler_params=pltpu.CompilerParams(vmem_limit_bytes=24 << 20),
         name="edge",
@@ -388,16 +459,17 @@
     sums, grown, scale = pl.pallas_call(
         middle_kernel,
         out_shape=(window, window, splat),
-        in_specs=[SMEM, HBM] + [VMEM] * 4,
+        in_specs=[SMEM, HBM] + [VMEM] * 7,
         out_specs=(VMEM,) * 3,
+        input_output_aliases={6: 0, 7: 1, 8: 2},
         scratch_shapes=[
-            pltpu.VMEM((CAP - 2, TILE, TILE), BF16),
+            pltpu.VMEM((TILE, TILE), BF16),
             window,
-            pltpu.SemaphoreType.DMA((CAP - 2,)),
+            pltpu.SemaphoreType.DMA,
         ],
         compiler_params=pltpu.CompilerParams(vmem_limit_bytes=24 << 20),
         name="middle",
-    )(info, in_hbm(contacts), edge, diagonal, first, spill)
+    )(info, in_hbm(contacts), edge, diagonal, first, spill, sums, grown, scale)
     raw, part, near, far, sent = pl.pallas_call(
         second_kernel,
         out_shape=(window, window, long, long, pltpu.VMEM((DEVICES, 128), F32)),
@@ -440,7 +512,7 @@
             window,
             pltpu.VMEM((CAP, TILE, 128), F32),
             pltpu.SemaphoreType.DMA((SLOTS - KEPT,)),
-            pltpu.SemaphoreType.DMA((SLOTS,)),
+            pltpu.SemaphoreType.DMA((SLOTS, HALVES)),
             pltpu.SemaphoreType.DMA((2,)),
         ],
         compiler_params=pltpu.CompilerParams(vmem_limit_bytes=32 << 20),

time: 42 us -> 41.6 us (level)
  no operation moved by 1% of the time
where the time goes in v4:
time: 41.6 us; the launch traced here: 41.3 us
  starting transfers between devices  24.5 us (59%)
  waiting for transfers between devices  8.65 us (21%)
  Pallas kernels  7.48 us (18%)
  between operations  0.7 us (2%)
    all_to_all x1, starting transfers between devices, shards(): everyone = lax.all_to_all(sent, 'dev', 0, 0, tiled=True)  14.9 us
    ppermute x2, waiting for transfers between devices, shards(): far = lax.ppermute(far, 'dev', far_pairs)  6.21 us
    ppermute x2, starting transfers between devices, shards(): near = lax.ppermute(near, 'dev', near_pairs)  5.83 us
    ppermute x2, starting transfers between devices, shards(): far = lax.ppermute(far, 'dev', far_pairs)  3.82 us
    pallas_call x1, Pallas kernels, shards(): pl.pallas_call(factor_kernel, out_shape=(pltpu.VMEM((KEPT, TILE, TILE), B...  2.99 us
    all_to_all x1, waiting for transfers between devices, shards(): everyone = lax.all_to_all(sent, 'dev', 0, 0, tiled=True)  2.43 us
    pallas_call x1, Pallas kernels, shards(): pl.pallas_call(edge_kernel, out_shape=(pltpu.VMEM((CAP + 1, TILE, TILE),...  1.88 us
    pallas_call x1, Pallas kernels, shards(): pl.pallas_call(last_kernel, out_shape=(jax.ShapeDtypeStruct((1, CAP * TIL...  1.38 us
  transfers between devices with their start and end apart: 5, of which 3 were waited for; matrix products, arithmetic and copies ran while one was open for 0% of the time, Pallas kernels for 7%

profile of v4, /device:TPU:1, one launch (start us, length us, event | category | flops | bytes accessed | tf_op | source)
XLA Modules:
  0.0 41.3 jit_solution(8465968659065869197)
XLA Ops:
  0.6 1.9 %edge.1 = (bf16[5,512,512]{2,1,0:T(8,128)(2,1)S(1)}, bf16[2,512,512]{2,1,0:T(8,128)(2,1)S(1)}, f32[1,512]{1,0:T(1,128)S(1)}, f32[1,512]{1,0:T(1,128)S(1)}, f32[1...) custom-call(bf16[8,512,512]{2,1,0:T(8,128)(2,1)} %c_hbm.7, ...), custom_call_target="tpu_custom_call" | custom-call | tf_op jit(solution)/shard_map/edge/pallas_call | solution.py:436
  2.5 3.6 %collective-permute-start = (f32[1,512]{1,0:T(1,128)S(1)}, f32[1,512]{1,0:T(1,128)S(1)}, u32[]{:S(2)}, u32[]{:S(2)}) collective-permute-start(f32[1,512]{1,0:T(1,128)S(1)} %get-tuple-element.37), channel_id=1, source_target_pairs={{0,1},{1,0},{2,3},{3,2},{4,5},{5,4},{6,7},{7,6},{8,9},{9,8},{10,11... | collective-permute-start | bytes 6152 | tf_op jit(solution)/shard_map/ppermute | solution.py:458
  6.1 1.9 %collective-permute-start.1 = (f32[1,512]{1,0:T(1,128)S(1)}, f32[1,512]{1,0:T(1,128)S(1)}, u32[]{:S(2)}, u32[]{:S(2)}) collective-permute-start(f32[1,512]{1,0:T(1,128)S(1)} %get-tuple-element.38), channel_id=1, source_target_pairs={{1,2},{2,1},{3,4},{4,3},{5,6},{6,5},{7,8},{8,7},{9,10},{10,9},{11,... | collective-permute-start | bytes 6152 | tf_op jit(solution)/shard_map/ppermute | solution.py:457
  8.1 0.0 collective-permute-done.near_in
  8.1 2.9 %collective-permute-done.1.far_in = f32[1,512]{1,0:T(1,128)S(1)} collective-permute-done((f32[1,512]{1,0:T(1,128)S(1)}, f32[1,512]{1,0:T(1,128)S(1)}, u32[]{:S(2)}, u32[]{:S(2)}) %collective-permute-start.1) | collective-permute-done | bytes 2080 | tf_op jit(solution)/shard_map/ppermute | solution.py:457
  11.0 1.2 %second.1 = (f32[8,512]{1,0:T(8,128)S(1)}, f32[8,512]{1,0:T(8,128)S(1)}, f32[1,640]{1,0:T(1,128)S(1)}, f32[1,640]{1,0:T(1,128)S(1)}, f32[256,128]{1,0:T(8,128)}) custom-call(s32[29]{0:T(128)S(4)} %get-tuple-element.26.info_ref, bf16[5,512,512]{2,1,0:T(8,128)(2,1)S(1)} %get-tuple-element.27.edge, f32[8,512]{1,0:T(8,128)S(1)} %get-tuple-element.34.sums_ref, ...), custom_call_target="tpu_custom_call" | custom-call | tf_op jit(solution)/shard_map/second/pallas_call | solution.py:473
  12.2 14.9 %all-to-all-start = ((f32[256,1,128]{2,1,0:T(1,128)}), f32[256,1,128]{2,1,0:T(1,128)S(1)}, u32[]{:S(2)}, u32[]{:S(2)}) async-start(f32[256,1,128]{2,1,0:T(1,128)} %bitcast.1), calls=%async_computation | async-start | bytes 262144 | tf_op jit(solution)/shard_map/all_to_all | solution.py:484
  27.1 2.2 %collective-permute-start.2 = (f32[1,640]{1,0:T(1,128)S(1)}, f32[1,640]{1,0:T(1,128)S(1)}, u32[]{:S(2)}, u32[]{:S(2)}) collective-permute-start(f32[1,640]{1,0:T(1,128)S(1)} %get-tuple-element.42), channel_id=1, source_target_pairs={{0,1},{1,0},{2,3},{3,2},{4,5},{5,4},{6,7},{7,6},{8,9},{9,8},{10,11... | collective-permute-start | bytes 7688 | tf_op jit(solution)/shard_map/ppermute | solution.py:483
  29.3 1.9 %collective-permute-start.3 = (f32[1,640]{1,0:T(1,128)S(1)}, f32[1,640]{1,0:T(1,128)S(1)}, u32[]{:S(2)}, u32[]{:S(2)}) collective-permute-start(f32[1,640]{1,0:T(1,128)S(1)} %get-tuple-element.43), channel_id=1, source_target_pairs={{1,2},{2,1},{3,4},{4,3},{5,6},{6,5},{7,8},{8,7},{9,10},{10,9},{11,... | collective-permute-start | bytes 7688 | tf_op jit(solution)/shard_map/ppermute | solution.py:482
  31.2 0.0 collective-permute-done.2.near_in
  31.3 3.3 %collective-permute-done.3.far_in = f32[1,640]{1,0:T(1,128)S(1)} collective-permute-done((f32[1,640]{1,0:T(1,128)S(1)}, f32[1,640]{1,0:T(1,128)S(1)}, u32[]{:S(2)}, u32[]{:S(2)}) %collective-permute-start.3) | collective-permute-done | bytes 2592 | tf_op jit(solution)/shard_map/ppermute | solution.py:482
  34.5 3.0 %factor.1 = (bf16[5,512,512]{2,1,0:T(8,128)(2,1)S(1)}, f32[8,512]{1,0:T(8,128)S(1)}, f32[512,8]{1,0:T(8,128)S(1)}, f32[8,512]{1,0:T(8,128)S(1)}, bf16[8,512,512]{2,1,0:T(8,128)(2,1)}) custom-call(s32[29]{0:T(128)S(4)} %get-tuple-element.26.info_ref, bf16[8,512,512]{2,1,0:T(8,128)(2,1)} %c_hbm.7, f32[8,512]{1,0:T(8,128)S(1)} %get-tuple-element.40.raw_ref, ...), custom_call_target="tpu_custom_call" | custom-call | tf_op jit(solution)/shard_map/factor/pallas_call | solution.py:486
  37.5 2.4 %all-to-all-done = f32[256,1,128]{2,1,0:T(1,128)S(1)} async-done(((f32[256,1,128]{2,1,0:T(1,128)}), f32[256,1,128]{2,1,0:T(1,128)S(1)}, u32[]{:S(2)}, u32[]{:S(2)}) %all-to-all-start) | async-done | bytes 131104 | tf_op jit(solution)/shard_map/all_to_all | solution.py:484
  40.0 1.4 %last.1 = (f32[1,2048]{1,0:T(1,128)}, f32[1,2048]{1,0:T(1,128)}, bf16[8,512,512]{2,1,0:T(8,128)(2,1)}) custom-call(s32[29]{0:T(128)S(4)} %get-tuple-element.26.info_ref, f32[256,128]{1,0:T(8,128)S(1)} %bitcast.4, bf16[8,512,512]{2,1,0:T(8,128)(2,1)} %c_hbm.7, bf16[5,512,512]{2,1,0:T(8,128)(2,1)S(1)} %get-tuple-element.44.kept, ...), custom_call_target="tpu_custom_call", output_to_operand_aliasing={{2}: (9, {})} | custom-call | tf_op jit(solution)/shard_map/last/pallas_call | solution.py:497
  (1 shorter events, 0.0 us)
Async XLA Ops:
  2.5 5.5 %collective-permute-start = (f32[1,512]{1,0:T(1,128)S(1)}, f32[1,512]{1,0:T(1,128)S(1)}, u32[]{:S(2)}, u32[]{:S(2)}) collective-permute-start(f32[1,512]{1,0:T(1,128)S(1)} %get-tuple-element.37), channel_id=1, source_target_pairs={{0,1},{1,0},{2,3},{3,2},{4,5},{5,4},{6,7},{7,6},{8,9},{9,8},{10,11... | collective-permute-start | bytes 6152 | tf_op jit(solution)/shard_map/ppermute | solution.py:458
  6.1 4.9 %collective-permute-start.1 = (f32[1,512]{1,0:T(1,128)S(1)}, f32[1,512]{1,0:T(1,128)S(1)}, u32[]{:S(2)}, u32[]{:S(2)}) collective-permute-start(f32[1,512]{1,0:T(1,128)S(1)} %get-tuple-element.38), channel_id=1, source_target_pairs={{1,2},{2,1},{3,4},{4,3},{5,6},{6,5},{7,8},{8,7},{9,10},{10,9},{11,... | collective-permute-start | bytes 6152 | tf_op jit(solution)/shard_map/ppermute | solution.py:457
  12.2 27.7 %all-to-all-start = ((f32[256,1,128]{2,1,0:T(1,128)}), f32[256,1,128]{2,1,0:T(1,128)S(1)}, u32[]{:S(2)}, u32[]{:S(2)}) async-start(f32[256,1,128]{2,1,0:T(1,128)} %bitcast.1), calls=%async_computation | async-start | bytes 262144 | tf_op jit(solution)/shard_map/all_to_all | solution.py:484
  27.1 4.2 %collective-permute-start.2 = (f32[1,640]{1,0:T(1,128)S(1)}, f32[1,640]{1,0:T(1,128)S(1)}, u32[]{:S(2)}, u32[]{:S(2)}) collective-permute-start(f32[1,640]{1,0:T(1,128)S(1)} %get-tuple-element.42), channel_id=1, source_target_pairs={{0,1},{1,0},{2,3},{3,2},{4,5},{5,4},{6,7},{7,6},{8,9},{9,8},{10,11... | collective-permute-start | bytes 7688 | tf_op jit(solution)/shard_map/ppermute | solution.py:483
  29.3 5.2 %collective-permute-start.3 = (f32[1,640]{1,0:T(1,128)S(1)}, f32[1,640]{1,0:T(1,128)S(1)}, u32[]{:S(2)}, u32[]{:S(2)}) collective-permute-start(f32[1,640]{1,0:T(1,128)S(1)} %get-tuple-element.43), channel_id=1, source_target_pairs={{1,2},{2,1},{3,4},{4,3},{5,6},{6,5},{7,8},{8,7},{9,10},{10,9},{11,... | collective-permute-start | bytes 7688 | tf_op jit(solution)/shard_map/ppermute | solution.py:482
